TPU v7x, 32 devices: a whole 2x2x4 slice. The times are simulated.
32 devices in a mesh: row: 16 (over z, x, core), col: 2 (over y).
Axes of the slice: x: 2, y: 2, z: 4, core: 2. Of those that a mesh axis runs over, the one named last changes fastest.
Arguments:
- tokens: bfloat16 [9232, 1024], P('row', 'col'), may hold values from -6 to 6
- gain_one: float32 [1024], P('col'), may hold values from 0.5 to 1.5
- shift_one: float32 [1024], P('col'), may hold values from -2.5 to 2.5
- qkv_weight: bfloat16 [3, 1024, 1024], P(None, 'row', 'col'), may hold values from -0.1875 to 0.1875
- qv_bias: float32 [2, 1024], P(None, 'col'), may hold values from -1.5 to 1.5
- proj_weight: bfloat16 [1024, 1024], P('col', 'row'), may hold values from -2.5 to 2.5
- proj_bias: float32 [1024], P('col'), may hold values from -2.5 to 2.5
- gain_two: float32 [1024], P('col'), may hold values from 0.5 to 1.5
- shift_two: float32 [1024], P('col'), may hold values from -2.5 to 2.5
- up_weight: bfloat16 [1024, 4096], P('row', 'col'), may hold values from -0.1875 to 0.1875
- up_bias: float32 [4096], P('col'), may hold values from -2.5 to 2.5
- down_weight: bfloat16 [4096, 1024], P('col', 'row'), may hold values from -0.09375 to 0.09375
- down_bias: float32 [1024], P('col'), may hold values from -2.5 to 2.5
- grad_out: bfloat16 [9232, 1024], P('row', 'col'), may hold values from -6 to 6
Outputs:
- output: bfloat16 [9232, 1024], P('row', 'col')
- grad_tokens: float32 [9232, 1024], P('row', 'col')
- grad_gain_one: float32 [1024], P('col')
- grad_shift_one: float32 [1024], P('col')
- grad_qkv_weight: float32 [3, 1024, 1024], P(None, 'row', 'col')
- grad_qv_bias: float32 [2, 1024], P(None, 'col')
- grad_proj_weight: float32 [1024, 1024], P('col', 'row')
- grad_proj_bias: float32 [1024], P('col')
- grad_gain_two: float32 [1024], P('col')
- grad_shift_two: float32 [1024], P('col')
- grad_up_weight: float32 [1024, 4096], P('row', 'col')
- grad_up_bias: float32 [4096], P('col')
- grad_down_weight: float32 [4096, 1024], P('col', 'row')
- grad_down_bias: float32 [1024], P('col')
All inputs are finite; a program needn't handle non-finite values.
Results may differ from a plain program's by a relative error of at most 0.011.
Values may be sent and summed in bfloat16 or wider, within the bound.
A program may use at most 128 MiB of HBM per device.

v0:
```python
from functools import partial

import jax
import jax.numpy as jnp
from jax import lax
from jax.sharding import PartitionSpec as P

D = 1024
HD = 64
SEQ = 577


epsilon = 1e-06


def row_totals(first_term, second_term):
    return lax.psum((jnp.sum(first_term, axis=1), jnp.sum(second_term, axis=1)), "col")


def norm_forward(values, gain_value, shift_value, feature_width):
    row_total, squares = row_totals(values, values * values)
    center = row_total / feature_width
    spread = squares / feature_width - center * center
    inverse = lax.rsqrt(spread + epsilon)
    normed = (values - center[:, None]) * inverse[:, None]
    return (normed, inverse, normed * gain_value + shift_value)


def norm_backward(grad_in, normed, inverse, gain_value, feature_width):
    scaled = grad_in * gain_value
    row_total, cross_sum = row_totals(scaled, scaled * normed)
    return inverse[:, None] * (
        scaled - row_total[:, None] / feature_width - normed * (cross_sum[:, None] / feature_width)
    )


def spread_features(values):
    return lax.all_gather(values, "col", axis=1, tiled=True)


def sum_features(term):
    return lax.psum_scatter(term, "col", scatter_dimension=1, tiled=True)


def spread_grads(values):
    return lax.all_gather(values, "col", axis=1, tiled=True)


def sum_grads(term):
    return lax.psum_scatter(term, "col", scatter_dimension=1, tiled=True)


def attend(item_tuple, score_scale):
    query_part, key_part, value_part = item_tuple
    scores = score_scale * jnp.einsum(
        "qhe,khe->hqk", query_part, key_part, preferred_element_type=jnp.float32
    )
    largest = jnp.max(scores, axis=-1, keepdims=True)
    shifted = jnp.exp(scores - largest)
    row_total = jnp.sum(shifted, axis=-1, keepdims=True)
    weights_low = (shifted / row_total).astype(jnp.bfloat16)
    mixed_part = jnp.einsum(
        "hqk,khe->qhe", weights_low, value_part, preferred_element_type=jnp.float32
    )
    return (mixed_part.astype(jnp.bfloat16), (largest + jnp.log(row_total))[..., 0])


def attend_back(item_tuple, score_scale):
    query_part, key_part, value_part, grad_part, log_total = item_tuple
    scores = score_scale * jnp.einsum(
        "qhe,khe->hqk", query_part, key_part, preferred_element_type=jnp.float32
    )
    weights = jnp.exp(scores - log_total[..., None])
    weights_low = weights.astype(jnp.bfloat16)
    grad_value = jnp.einsum(
        "hqk,qhe->khe", weights_low, grad_part, preferred_element_type=jnp.float32
    )
    grad_weights = jnp.einsum(
        "qhe,khe->hqk", grad_part, value_part, preferred_element_type=jnp.float32
    )
    grad_scores = (
        weights * (grad_weights - jnp.sum(weights * grad_weights, axis=-1, keepdims=True))
    ).astype(jnp.bfloat16)
    grad_query = score_scale * jnp.einsum(
        "hqk,khe->qhe", grad_scores, key_part, preferred_element_type=jnp.float32
    )
    grad_key = score_scale * jnp.einsum(
        "hqk,qhe->khe", grad_scores, query_part, preferred_element_type=jnp.float32
    )
    return (grad_query, grad_key, grad_value)


def on_device(
    tokens,
    gain_one,
    shift_one,
    qkv_weight,
    qv_bias,
    proj_weight,
    proj_bias,
    gain_two,
    shift_two,
    up_weight,
    up_bias,
    down_weight,
    down_bias,
    grad_out,
):
    row_count = tokens.shape[0]
    local_width = tokens.shape[1]
    head_count = local_width // HD
    image_count = row_count // SEQ
    score_scale = HD ** (-0.5)

    def to_images(values):
        return values.reshape(image_count, SEQ, head_count, HD)

    qkv_full, proj_full, up_full, down_full = (
        lax.all_gather(qkv_weight, "row", axis=1, tiled=True),
        lax.all_gather(proj_weight, "row", axis=1, tiled=True),
        lax.all_gather(up_weight, "row", axis=0, tiled=True),
        lax.all_gather(down_weight, "row", axis=1, tiled=True),
    )
    x_value = tokens.astype(jnp.float32)
    normed_one, inverse_one, pre_one = norm_forward(x_value, gain_one, shift_one, D)
    input_one = spread_features(pre_one.astype(jnp.bfloat16))
    projected = jnp.einsum("td,jde->jte", input_one, qkv_full, preferred_element_type=jnp.float32)
    query_rows = (projected[0] + qv_bias[0]).astype(jnp.bfloat16)
    key_rows = projected[1].astype(jnp.bfloat16)
    value_rows = (projected[2] + qv_bias[1]).astype(jnp.bfloat16)
    mixed_heads, log_total = lax.map(
        partial(attend, score_scale=score_scale),
        (to_images(query_rows), to_images(key_rows), to_images(value_rows)),
    )
    mixed_heads = mixed_heads.reshape(row_count, local_width)
    branch_out = (
        sum_features(jnp.dot(mixed_heads, proj_full, preferred_element_type=jnp.float32))
        + proj_bias
    )
    hidden = x_value + branch_out
    normed_two, inverse_two, pre_two = norm_forward(hidden, gain_two, shift_two, D)
    input_two = spread_features(pre_two.astype(jnp.bfloat16))
    up_value = jnp.dot(input_two, up_full, preferred_element_type=jnp.float32) + up_bias
    activated = jax.nn.gelu(up_value, approximate=False).astype(jnp.bfloat16)
    down_value = (
        sum_features(jnp.dot(activated, down_full, preferred_element_type=jnp.float32)) + down_bias
    )
    output = (hidden + down_value).astype(jnp.bfloat16)
    qkv_back, proj_back, up_back, down_back = (
        lax.all_gather(qkv_weight, "row", axis=1, tiled=True),
        lax.all_gather(proj_weight, "row", axis=1, tiled=True),
        lax.all_gather(up_weight, "row", axis=0, tiled=True),
        lax.all_gather(down_weight, "row", axis=1, tiled=True),
    )
    upstream = grad_out.astype(jnp.float32)
    grad_down_bias = jnp.sum(upstream, axis=0)
    down_grads_full = spread_grads(grad_out)
    w_down_term = jnp.einsum(
        "tf,td->fd", activated, down_grads_full, preferred_element_type=jnp.float32
    )
    grad_down_weight = lax.psum_scatter(w_down_term, "row", scatter_dimension=1, tiled=True)
    grad_activated = jnp.einsum(
        "td,fd->tf", down_grads_full, down_back, preferred_element_type=jnp.float32
    )
    unused_value, gelu_pull = jax.vjp(
        lambda inner_value: jax.nn.gelu(inner_value, approximate=False), up_value
    )
    grad_up = gelu_pull(grad_activated)[0].astype(jnp.bfloat16)
    grad_up_bias = jnp.sum(grad_up, axis=0, dtype=jnp.float32)
    w_up_term = jnp.einsum("td,tf->df", input_two, grad_up, preferred_element_type=jnp.float32)
    grad_up_weight = lax.psum_scatter(w_up_term, "row", scatter_dimension=0, tiled=True)
    grad_input_two = sum_grads(
        jnp.einsum("tf,df->td", grad_up, up_back, preferred_element_type=jnp.float32)
    )
    grad_gain_two = jnp.sum(grad_input_two * normed_two, axis=0)
    grad_shift_two = jnp.sum(grad_input_two, axis=0)
    grad_hidden = upstream + norm_backward(grad_input_two, normed_two, inverse_two, gain_two, D)
    grad_branch = grad_hidden.astype(jnp.bfloat16)
    grad_proj_bias = jnp.sum(grad_branch, axis=0, dtype=jnp.float32)
    branch_grads_full = spread_grads(grad_branch)
    w_proj_term = jnp.einsum(
        "te,td->ed", mixed_heads, branch_grads_full, preferred_element_type=jnp.float32
    )
    grad_proj_weight = lax.psum_scatter(w_proj_term, "row", scatter_dimension=1, tiled=True)
    grad_mixed = jnp.einsum(
        "td,ed->te", branch_grads_full, proj_back, preferred_element_type=jnp.float32
    ).astype(jnp.bfloat16)
    grad_query, grad_key, grad_value = lax.map(
        partial(attend_back, score_scale=score_scale),
        (
            to_images(query_rows),
            to_images(key_rows),
            to_images(value_rows),
            to_images(grad_mixed),
            log_total,
        ),
    )
    grad_stack = jnp.stack(
        [
            grad_query.reshape(row_count, local_width),
            grad_key.reshape(row_count, local_width),
            grad_value.reshape(row_count, local_width),
        ]
    ).astype(jnp.bfloat16)
    grad_qv_bias = jnp.stack(
        [
            jnp.sum(grad_stack[0], axis=0, dtype=jnp.float32),
            jnp.sum(grad_stack[2], axis=0, dtype=jnp.float32),
        ]
    )
    w_qkv_term = jnp.einsum(
        "td,jte->jde", input_one, grad_stack, preferred_element_type=jnp.float32
    )
    grad_qkv_weight = lax.psum_scatter(w_qkv_term, "row", scatter_dimension=1, tiled=True)
    grad_input_one = sum_grads(
        jnp.einsum("jte,jde->td", grad_stack, qkv_back, preferred_element_type=jnp.float32)
    )
    grad_gain_one = jnp.sum(grad_input_one * normed_one, axis=0)
    grad_shift_one = jnp.sum(grad_input_one, axis=0)
    grad_tokens = grad_hidden + norm_backward(grad_input_one, normed_one, inverse_one, gain_one, D)
    small_sums = lax.psum(
        (
            grad_gain_one,
            grad_shift_one,
            grad_qv_bias,
            grad_proj_bias,
            grad_gain_two,
            grad_shift_two,
            grad_up_bias,
            grad_down_bias,
        ),
        "row",
    )
    return (
        output,
        grad_tokens,
        small_sums[0],
        small_sums[1],
        grad_qkv_weight,
        small_sums[2],
        grad_proj_weight,
        small_sums[3],
        small_sums[4],
        small_sums[5],
        grad_up_weight,
        small_sums[6],
        grad_down_weight,
        small_sums[7],
    )


def solution(mesh):
    return jax.shard_map(
        on_device,
        mesh=mesh,
        in_specs=(
            P("row", "col"),
            P("col"),
            P("col"),
            P(None, "row", "col"),
            P(None, "col"),
            P("col", "row"),
            P("col"),
            P("col"),
            P("col"),
            P("row", "col"),
            P("col"),
            P("col", "row"),
            P("col"),
            P("row", "col"),
        ),
        out_specs=(
            P("row", "col"),
            P("row", "col"),
            P("col"),
            P("col"),
            P(None, "row", "col"),
            P(None, "col"),
            P("col", "row"),
            P("col"),
            P("col"),
            P("col"),
            P("row", "col"),
            P("col"),
            P("col", "row"),
            P("col"),
        ),
        check_vma=False,
    )
```

profile of v0, /device:TPU:0, one launch (start us, length us, event | category | flops | bytes accessed | tf_op | source)
XLA Modules:
  0.0 978.8 jit_solution(1349739847183167165)
XLA Ops:
  8.6 6.0 all-reduce.5
  15.1 2.2 fusion.25
  19.8 22.4 %all-gather.9.cloned.1.call-done = bf16[577,1024]{1,0:T(8,128)(2,1)} async-done(((bf16[577,512]{1,0:T(8,128)(2,1)}), bf16[577,1024]{1,0:T(8,128)(2,1)}) %all-gather.9.cloned.1.call-update) | async-done | bytes 1181712 | tf_op jit(solution)/shard_map/all_gather | solution.py:38
  42.2 47.7 %all-gather.11.cloned.1.call-done = bf16[3,1024,512]{2,1,0:T(8,128)(2,1)} async-done(((bf16[3,64,512]{2,1,0:T(8,128)(2,1)}), bf16[3,1024,512]{2,1,0:T(8,128)(2,1)}) %all-gather.11.cloned.1.call-update) | async-done | bytes 3145744 | tf_op jit(solution)/shard_map/all_gather | solution.py:119
  89.9 4.3 convolution_bitcast_fusion.1
  96.2 2.1 multiply_reduce_fusion.1
  98.4 2.0 fusion
  100.4 2.4 copy-done
  102.8 1.7 copy.54
  104.5 8.5 fusion.18
  113.0 15.3 %all-gather.13.cloned.1.call-done = bf16[512,1024]{0,1:T(8,128)(2,1)} async-done(((bf16[512,64]{0,1:T(8,128)(2,1)}), bf16[512,1024]{0,1:T(8,128)(2,1)}) %all-gather.13.cloned.1.call-update) | async-done | bytes 1048592 | tf_op jit(solution)/shard_map/all_gather | solution.py:120
  128.3 3.9 fusion.43
  132.9 33.6 %reduce-scatter.8.cloned.1.call-done = f32[577,512]{1,0:T(8,128)} async-done(((f32[577,1024]{1,0:T(8,128)}), f32[577,512]{1,0:T(8,128)}) %reduce-scatter.8.cloned.1.call-update) | async-done | bytes 1181712 | tf_op jit(solution)/shard_map/reduce_scatter | solution.py:42
  168.1 5.0 all-reduce.4
  175.8 43.1 %all-gather.17.cloned.1.call-done = bf16[1024,2048]{1,0:T(8,128)(2,1)} async-done(((bf16[64,2048]{1,0:T(8,128)(2,1)}), bf16[1024,2048]{1,0:T(8,128)(2,1)}) %all-gather.17.cloned.1.call-update) | async-done | bytes 4194320 | tf_op jit(solution)/shard_map/all_gather | solution.py:121
  218.9 23.5 %all-gather.15.cloned.1.call-done = bf16[577,1024]{1,0:T(8,128)(2,1)} async-done(((bf16[577,512]{1,0:T(8,128)(2,1)}), bf16[577,1024]{1,0:T(8,128)(2,1)}) %all-gather.15.cloned.1.call-update) | async-done | bytes 1181712 | tf_op jit(solution)/shard_map/all_gather | solution.py:38
  242.4 7.3 fusion.44
  249.8 17.2 %all-gather.21.cloned.1.call-done = bf16[577,1024]{1,0:T(8,128)(2,1)} async-done(((bf16[577,512]{1,0:T(8,128)(2,1)}), bf16[577,1024]{1,0:T(8,128)(2,1)}) %all-gather.21.cloned.1.call-update) | async-done | bytes 1181712 | tf_op jit(solution)/shard_map/all_gather | solution.py:46
  266.9 52.6 %all-gather.19.cloned.1.call-done = bf16[2048,1024]{0,1:T(8,128)(2,1)} async-done(((bf16[2048,64]{0,1:T(8,128)(2,1)}), bf16[2048,1024]{0,1:T(8,128)(2,1)}) %all-gather.19.cloned.1.call-update) | async-done | bytes 4194320 | tf_op jit(solution)/shard_map/all_gather | solution.py:122
  319.5 17.0 %convert_reduce_fusion = (f32[2048]{0:T(1024)S(1)}, bf16[577,2048]{1,0:T(8,128)(2,1)S(1)}, f32[577,2048]{1,0:T(8,128)}) fusion(f32[577,2048]{1,0:T(8,128)} %fusion.44, f32[2048]{0:T(1024)S(1)} %copy-done.20, bf16[577,1024]{1,0:T(8,128)(2,1)} %all-gather.21.cloned.1.call-done, bf16[2048,1024]{0,1:T(8,128)(2,1)} %all-gather.19.cloned.1.call-done), kind=kOutput, calls=%fused_computation.14 | convolution fusion | flops 2508738560 | bytes 17209344 | tf_op jit(solution)/shard_map/td,fd->tf/dot_general | solution.py:162
  337.9 4.1 fusion.46
  342.1 5.1 multiply_convert_fusion.1
  348.7 4.1 fusion.45
  352.9 22.9 %reduce-scatter.12.cloned.1.call-done = f32[577,512]{1,0:T(8,128)} async-done(((f32[577,1024]{1,0:T(8,128)}), f32[577,512]{1,0:T(8,128)}) %reduce-scatter.12.cloned.1.call-update) | async-done | bytes 1181712 | tf_op jit(solution)/shard_map/reduce_scatter | solution.py:50
  375.9 1.9 multiply_reduce_fusion.2
  377.7 5.2 all-reduce.3
  382.9 30.2 %reduce-scatter.10.cloned.1.call-done = f32[577,512]{1,0:T(8,128)} async-done(((f32[577,1024]{1,0:T(8,128)}), f32[577,512]{1,0:T(8,128)}) %reduce-scatter.10.cloned.1.call-update) | async-done | bytes 1181712 | tf_op jit(solution)/shard_map/reduce_scatter | solution.py:42
  413.2 3.7 convert_reduce_fusion.5
  416.9 23.0 %all-gather.23.cloned.1.call-done = bf16[577,1024]{1,0:T(8,128)(2,1)} async-done(((bf16[577,512]{1,0:T(8,128)(2,1)}), bf16[577,1024]{1,0:T(8,128)(2,1)}) %all-gather.23.cloned.1.call-update) | async-done | bytes 1181712 | tf_op jit(solution)/shard_map/all_gather | solution.py:46
  440.0 2.4 convolution_convert_fusion
  442.7 6.7 fusion.15
  449.4 8.6 multiply_reduce_fusion
  458.0 6.2 multiply_convert_fusion
  464.3 1.9 fusion.14
  468.1 6.2 convolution_bitcast_fusion
  474.3 9.4 copy.65
  484.7 5.6 convolution_bitcast_fusion.2
  490.6 3.7 fusion.47
  494.4 7.5 fusion.49
  503.2 7.4 fusion.48
  512.8 141.1 %all-reduce.8.cloned.1.call-done = f32[3,1024,512]{2,0,1:T(4,128)} async-done(((f32[3,1024,512]{2,0,1:T(4,128)}), f32[3,1024,512]{2,0,1:T(4,128)}) %all-reduce.8.cloned.1.call-update) | async-done | bytes 6291472
  655.9 35.3 %reduce-scatter.14.cloned.1.call-done = f32[577,512]{1,0:T(8,128)} async-done(((f32[577,1024]{1,0:T(8,128)}), f32[577,512]{1,0:T(8,128)}) %reduce-scatter.14.cloned.1.call-update) | async-done | bytes 1181712 | tf_op jit(solution)/shard_map/reduce_scatter | solution.py:50
  691.2 1.9 fusion.30
  693.1 61.5 %all-reduce.1 = (f32[512]{0:T(512)}, f32[512]{0:T(512)}, f32[2,512]{1,0:T(2,128)}, f32[512]{0:T(512)}, f32[512]{0:T(512)}, /*index=5*/f32[512]{0:T(512)}, f32[2048]{0:T(1024)}, f32[512]{0:T(512)}) all-reduce(f32[512]{0:T(512)S(1)} %get-tuple-element.103, f32[512]{0:T(512)S(1)} %get-tuple-element.108, ...), channel_id=1, replica_groups=mesh['row'=16,'col'=2] {'row'}, use_global_device_ids=true, to_apply=%region_24.25 | all-reduce | flops 6144 | bytes 49152 | tf_op jit(solution)/shard_map/psum | solution.py:221
  754.6 5.0 all-reduce.2
  759.6 2.7 fusion.29
  762.3 101.9 %reduce-scatter.20.cloned.1.call-done = f32[2048,64]{0,1:T(8,128)} async-done(((f32[2048,1024]{0,1:T(8,128)}), f32[2048,64]{0,1:T(8,128)}) %reduce-scatter.20.cloned.1.call-update) | async-done | bytes 524304 | tf_op jit(solution)/shard_map/reduce_scatter | solution.py:161
  864.2 107.6 %reduce-scatter.18.cloned.1.call-done = f32[64,2048]{1,0:T(8,128)} async-done(((f32[1024,2048]{1,0:T(8,128)}), f32[64,2048]{1,0:T(8,128)}) %reduce-scatter.18.cloned.1.call-update) | async-done | bytes 524304 | tf_op jit(solution)/shard_map/reduce_scatter | solution.py:171
  (126 shorter events, 22.8 us)
Async XLA Ops:
  7.2 35.0 %all-gather.9.cloned.1.call-start = ((), (), s32[]{:S(2)}) async-start(), calls=%async_computation.7 | async-start | bytes 1794048 | tf_op jit(solution)/shard_map/all_gather | solution.py:38
  14.5 0.6 copy-start.14
  17.3 72.6 %all-gather.11.cloned.1.call-start = ((), (), s32[]{:S(2)}) async-start(), calls=%async_computation.8 | async-start | bytes 3342336 | tf_op jit(solution)/shard_map/all_gather | solution.py:119
  18.1 110.2 %all-gather.13.cloned.1.call-start = ((), (), s32[]{:S(2)}) async-start(), calls=%async_computation.9 | async-start | bytes 1114112 | tf_op jit(solution)/shard_map/all_gather | solution.py:120
  18.8 147.7 %reduce-scatter.8.cloned.1.call-start = ((), (), s32[]{:S(2)}) async-start(), calls=%async_computation.10 | async-start | bytes 3588096 | tf_op jit(solution)/shard_map/reduce_scatter | solution.py:42
  95.8 2.5 copy-start.3
  98.4 4.4 copy-start
  104.5 8.5 copy-start.5
  128.3 38.2 %copy-start.1 = (bf16[577,512]{1,0:T(8,128)(2,1)S(1)}, bf16[577,512]{1,0:T(8,128)(2,1)}, u32[]{:S(2)}) copy-start(bf16[577,512]{1,0:T(8,128)(2,1)} %param.14) | copy-start | bytes 1772548
  128.3 38.2 %copy-start.22 = (f32[512]{0:T(512)S(1)}, f32[512]{0:T(512)}, u32[]{:S(2)}) copy-start(f32[512]{0:T(512)} %param.20) | copy-start | bytes 6148
  132.2 40.9 %copy-start.18 = (f32[512]{0:T(512)S(1)}, f32[512]{0:T(512)}, u32[]{:S(2)}) copy-start(f32[512]{0:T(512)} %param.21) | copy-start | bytes 6148
  132.2 40.9 %copy-start.23 = (f32[512]{0:T(512)S(1)}, f32[512]{0:T(512)}, u32[]{:S(2)}) copy-start(f32[512]{0:T(512)} %param.22) | copy-start | bytes 6148
  132.2 86.7 %all-gather.17.cloned.1.call-start = ((), (), s32[]{:S(2)}) async-start(), calls=%async_computation.12 | async-start | bytes 4456448 | tf_op jit(solution)/shard_map/all_gather | solution.py:121
  132.8 109.6 %all-gather.15.cloned.1.call-start = ((), (), s32[]{:S(2)}) async-start(), calls=%async_computation.11 | async-start | bytes 1794048 | tf_op jit(solution)/shard_map/all_gather | solution.py:38
  174.3 92.7 %all-gather.21.cloned.1.call-start = ((), (), s32[]{:S(2)}) async-start(), calls=%async_computation.15 | async-start | bytes 1794048 | tf_op jit(solution)/shard_map/all_gather | solution.py:46
  175.0 144.5 %all-gather.19.cloned.1.call-start = ((), (), s32[]{:S(2)}) async-start(), calls=%async_computation.13 | async-start | bytes 4456448 | tf_op jit(solution)/shard_map/all_gather | solution.py:122
  175.8 143.8 %copy-start.20 = (f32[2048]{0:T(1024)S(1)}, f32[2048]{0:T(1024)}, u32[]{:S(2)}) copy-start(f32[2048]{0:T(1024)} %param.24) | copy-start | bytes 24580
  175.8 200.1 %reduce-scatter.12.cloned.1.call-start = ((), (), s32[]{:S(2)}) async-start(), calls=%async_computation.16 | async-start | bytes 3588096 | tf_op jit(solution)/shard_map/reduce_scatter | solution.py:50
  319.5 18.4 %copy-start.24 = (bf16[1024,2048]{1,0:T(8,128)(2,1)S(1)}, bf16[1024,2048]{1,0:T(8,128)(2,1)}, u32[]{:S(2)}) copy-start(bf16[1024,2048]{1,0:T(8,128)(2,1)} %all-gather.17.cloned.1.call-done) | copy-start | bytes 12582916
  336.5 1.4 copy-start.29
  342.0 71.1 %reduce-scatter.10.cloned.1.call-start = ((), (), s32[]{:S(2)}) async-start(), calls=%async_computation.14 | async-start | bytes 3588096 | tf_op jit(solution)/shard_map/reduce_scatter | solution.py:42
  342.1 6.6 copy-start.25
  347.2 1.5 copy-start.9
  352.9 60.3 %copy-start.8 = (bf16[577,512]{1,0:T(8,128)(2,1)S(1)}, bf16[577,512]{1,0:T(8,128)(2,1)}, u32[]{:S(2)}) copy-start(bf16[577,512]{1,0:T(8,128)(2,1)} %param.27) | copy-start | bytes 1772548
  352.9 60.3 %copy-start.21 = (f32[512]{0:T(512)S(1)}, f32[512]{0:T(512)}, u32[]{:S(2)}) copy-start(f32[512]{0:T(512)} %param.26) | copy-start | bytes 6148
  352.9 87.1 %all-gather.23.cloned.1.call-start = ((), (), s32[]{:S(2)}) async-start(), calls=%async_computation.17 | async-start | bytes 1794048 | tf_op jit(solution)/shard_map/all_gather | solution.py:46
  416.9 237.0 %all-reduce.8.cloned.1.call-start = ((), (), s32[]{:S(2)}) async-start(), calls=%async_computation.22 | async-start | bytes 16777216
  442.6 6.7 copy-start.6
  442.6 15.4 %slice-start = ((s8[11960320]{0:T(1024)(128)(4,1)}), s8[4194304]{0:T(1024)(128)(4,1)S(1)}, s32[]{:S(2)}) async-start(s8[11960320]{0:T(1024)(128)(4,1)} %bitcast.58), calls=%async_computation.23 | async-start | bytes 8388608
  442.7 15.4 %slice-start.1 = ((s8[11960320]{0:T(1024)(128)(4,1)}), s8[4194304]{0:T(1024)(128)(4,1)S(1)}, s32[]{:S(2)}) async-start(s8[11960320]{0:T(1024)(128)(4,1)} %bitcast.58), calls=%async_computation.24 | async-start | bytes 8388608
  449.4 8.7 slice-start.2
  464.3 1.9 copy-start.4
  467.8 6.4 copy-start.11
  468.1 6.2 copy-start.13
  483.6 1.1 copy-start.12
  483.7 7.0 copy-start.10
  483.7 207.5 %reduce-scatter.14.cloned.1.call-start = ((), (), s32[]{:S(2)}) async-start(), calls=%async_computation.18 | async-start | bytes 3588096 | tf_op jit(solution)/shard_map/reduce_scatter | solution.py:50
  490.3 4.1 copy-start.27
  490.3 272.0 %reduce-scatter.16.cloned.1.call-start = ((), (), s32[]{:S(2)}) async-start(), calls=%async_computation.19 | async-start | bytes 2228224 | tf_op jit(solution)/shard_map/reduce_scatter | solution.py:184
  494.3 369.8 %reduce-scatter.20.cloned.1.call-start = ((), (), s32[]{:S(2)}) async-start(), calls=%async_computation.21 | async-start | bytes 8912896 | tf_op jit(solution)/shard_map/reduce_scatter | solution.py:161
  501.9 1.3 copy-start.26
  501.9 469.9 %reduce-scatter.18.cloned.1.call-start = ((), (), s32[]{:S(2)}) async-start(), calls=%async_computation.20 | async-start | bytes 8912896 | tf_op jit(solution)/shard_map/reduce_scatter | solution.py:171
  510.5 0.7 copy-start.28
  510.6 180.6 %copy-start.2 = (bf16[577,512]{1,0:T(8,128)(2,1)S(1)}, bf16[577,512]{1,0:T(8,128)(2,1)}, u32[]{:S(2)}) copy-start(bf16[577,512]{1,0:T(8,128)(2,1)} %param.14) | copy-start | bytes 1772548
  510.6 180.6 %copy-start.15 = (f32[577]{0:T(1024)S(1)}, f32[577]{0:T(1024)}, u32[]{:S(2)}) copy-start(f32[577]{0:T(1024)} %copy-done.14) | copy-start | bytes 6928
  510.6 180.6 %copy-start.17 = (f32[577]{0:T(1024)S(1)}, f32[577]{0:T(1024)}, u32[]{:S(2)}) copy-start(f32[577]{0:T(1024)} %copy-done.16) | copy-start | bytes 6928
  510.6 180.6 %copy-start.19 = (f32[512]{0:T(512)S(1)}, f32[512]{0:T(512)}, u32[]{:S(2)}) copy-start(f32[512]{0:T(512)} %param.15) | copy-start | bytes 6148
  510.6 249.0 %copy-start.7 = (f32[577,512]{1,0:T(8,128)S(1)}, f32[577,512]{1,0:T(8,128)}, u32[]{:S(2)}) copy-start(f32[577,512]{1,0:T(8,128)} %get-tuple-element.136) | copy-start | bytes 3545092
  (1 other events, 0.6 us)
Sparse Core Ops, SparseCore 0:
  17.5 24.6 all-gather.8
  44.4 45.4 all-gather.10
  92.1 36.1 all-gather.12
  132.4 34.1 reduce-scatter.7
  168.5 50.3 all-gather.16
  220.9 21.4 all-gather.14
  244.0 22.9 all-gather.20
  269.1 50.3 all-gather.18
  342.1 33.6 reduce-scatter.11
  378.0 35.1 reduce-scatter.9
  417.0 22.9 all-gather.22
  483.8 170.0 all-reduce.7
  656.1 34.9 reduce-scatter.13
  695.3 61.8 reduce-scatter.15
  761.7 102.3 reduce-scatter.19
  868.7 103.0 reduce-scatter.17
where the time goes:
time: 988 us; the launch traced here: 979 us
  waiting for transfers between devices  721 us (73%)
  matrix products  102 us (10%)
  blocking collectives  82.6 us (8%)
  other arithmetic  30.2 us (3%)
  local copies, waits for them, and re-layouts  26.3 us (3%)
  between operations  15.5 us (2%)
    unnamed x17, waiting for transfers between devices  144 us
    reduce_scatter x1, waiting for transfers between devices, on_device(): lax.psum_scatter(w_up_term, 'row', scatter_dimension=0, tiled=True)  108 us
    reduce_scatter x1, waiting for transfers between devices, on_device(): lax.psum_scatter(w_down_term, 'row', scatter_dimension=1, tiled=True)  102 us
    reduce_scatter x2, waiting for transfers between devices, sum_features(): return lax.psum_scatter(term, 'col', scatter_dimension=1, tiled=True)  63.9 us
    psum x1, blocking collectives, on_device(): lax.psum((grad_gain_one, grad_shift_one, grad_qv_bias, grad_proj_bias, gr...  61.5 us
    reduce_scatter x2, waiting for transfers between devices, sum_grads(): return lax.psum_scatter(term, 'col', scatter_dimension=1, tiled=True)  58.2 us
    all_gather x1, waiting for transfers between devices, on_device(): lax.all_gather(down_weight, 'row', axis=1, tiled=True)  52.6 us
    all_gather x1, waiting for transfers between devices, on_device(): lax.all_gather(qkv_weight, 'row', axis=1, tiled=True)  47.7 us
  transfers between devices with their start and end apart: 16, of which 15 were waited for; matrix products, arithmetic and copies ran while one was open for 8% of the time, Pallas kernels for 0%

commit v1 on v0

--- a/solution.py
+++ b/solution.py
@@ -34,20 +34,58 @@
     )
 
 
-def spread_features(values):
-    return lax.all_gather(values, "col", axis=1, tiled=True)
-
-
-def sum_features(term):
-    return lax.psum_scatter(term, "col", scatter_dimension=1, tiled=True)
-
-
-def spread_grads(values):
-    return lax.all_gather(values, "col", axis=1, tiled=True)
-
-
-def sum_grads(term):
-    return lax.psum_scatter(term, "col", scatter_dimension=1, tiled=True)
+def column_ring(shift):
+    count = lax.axis_size("col")
+    return [(i, (i + shift) % count) for i in range(count)]
+
+
+def spread(values):
+    count, here = lax.axis_size("col"), lax.axis_index("col")
+    width = values.shape[1]
+    out = jnp.zeros((values.shape[0], width * count), values.dtype)
+    out = lax.dynamic_update_slice(out, values, (0, here * width))
+    for shift in range(1, count):
+        got = lax.ppermute(values, "col", column_ring(shift))
+        out = lax.dynamic_update_slice(out, got, (0, ((here - shift) % count) * width))
+    return out
+
+
+def collect(term):
+    count, here = lax.axis_size("col"), lax.axis_index("col")
+    width = term.shape[1] // count
+    total = lax.dynamic_slice_in_dim(term, here * width, width, 1)
+    for shift in range(1, count):
+        block = lax.dynamic_slice_in_dim(term, ((here + shift) % count) * width, width, 1)
+        got = lax.ppermute(block.astype(jnp.bfloat16), "col", column_ring(shift))
+        total = total + got.astype(jnp.float32)
+    return total
+
+
+def gather_rows(block):
+    return lax.all_gather(block, "row", axis=0, tiled=True)
+
+
+def scatter_rows(term):
+    count = lax.axis_size("row")
+    chips = count // 2
+    pairs = [[i, i + 1] for i in range(0, count, 2)]
+    rings = [list(range(0, count, 2)), list(range(1, count, 2))]
+    rows, width = term.shape
+    term = term.reshape(chips, 2, rows // count, width).swapaxes(0, 1)
+    got = lax.all_to_all(term.astype(jnp.bfloat16), "row", 0, 0, axis_index_groups=pairs)
+    half = jnp.sum(got.astype(jnp.float32), axis=0).astype(jnp.bfloat16)
+    got = lax.all_to_all(half, "row", 0, 0, axis_index_groups=rings)
+    return jnp.sum(got.astype(jnp.float32), axis=0)
+
+
+def sum_small(parts):
+    flat = jnp.concatenate([part.reshape(-1) for part in parts])
+    flat = jnp.sum(lax.all_gather(flat, "row", axis=0), axis=0)
+    outs, start = [], 0
+    for part in parts:
+        outs.append(flat[start : start + part.size].reshape(part.shape))
+        start += part.size
+    return outs
 
 
 def attend(item_tuple, score_scale):
@@ -116,51 +154,45 @@
         return values.reshape(image_count, SEQ, head_count, HD)
 
     qkv_full, proj_full, up_full, down_full = (
-        lax.all_gather(qkv_weight, "row", axis=1, tiled=True),
-        lax.all_gather(proj_weight, "row", axis=1, tiled=True),
-        lax.all_gather(up_weight, "row", axis=0, tiled=True),
-        lax.all_gather(down_weight, "row", axis=1, tiled=True),
+        gather_rows(qkv_weight.swapaxes(0, 1).reshape(-1, 3 * local_width)),
+        gather_rows(proj_weight.T),
+        gather_rows(up_weight),
+        gather_rows(down_weight.T),
     )
     x_value = tokens.astype(jnp.float32)
     normed_one, inverse_one, pre_one = norm_forward(x_value, gain_one, shift_one, D)
-    input_one = spread_features(pre_one.astype(jnp.bfloat16))
-    projected = jnp.einsum("td,jde->jte", input_one, qkv_full, preferred_element_type=jnp.float32)
-    query_rows = (projected[0] + qv_bias[0]).astype(jnp.bfloat16)
-    key_rows = projected[1].astype(jnp.bfloat16)
-    value_rows = (projected[2] + qv_bias[1]).astype(jnp.bfloat16)
+    input_one = spread(pre_one.astype(jnp.bfloat16))
+    projected = jnp.dot(input_one, qkv_full, preferred_element_type=jnp.float32)
+    query_rows = (projected[:, :local_width] + qv_bias[0]).astype(jnp.bfloat16)
+    key_rows = projected[:, local_width : 2 * local_width].astype(jnp.bfloat16)
+    value_rows = (projected[:, 2 * local_width :] + qv_bias[1]).astype(jnp.bfloat16)
     mixed_heads, log_total = lax.map(
         partial(attend, score_scale=score_scale),
         (to_images(query_rows), to_images(key_rows), to_images(value_rows)),
     )
     mixed_heads = mixed_heads.reshape(row_count, local_width)
     branch_out = (
-        sum_features(jnp.dot(mixed_heads, proj_full, preferred_element_type=jnp.float32))
+        collect(jnp.einsum("te,de->td", mixed_heads, proj_full, preferred_element_type=jnp.float32))
         + proj_bias
     )
     hidden = x_value + branch_out
     normed_two, inverse_two, pre_two = norm_forward(hidden, gain_two, shift_two, D)
-    input_two = spread_features(pre_two.astype(jnp.bfloat16))
+    input_two = spread(pre_two.astype(jnp.bfloat16))
     up_value = jnp.dot(input_two, up_full, preferred_element_type=jnp.float32) + up_bias
     activated = jax.nn.gelu(up_value, approximate=False).astype(jnp.bfloat16)
     down_value = (
-        sum_features(jnp.dot(activated, down_full, preferred_element_type=jnp.float32)) + down_bias
+        collect(jnp.einsum("tf,df->td", activated, down_full, preferred_element_type=jnp.float32)) + down_bias
     )
     output = (hidden + down_value).astype(jnp.bfloat16)
-    qkv_back, proj_back, up_back, down_back = (
-        lax.all_gather(qkv_weight, "row", axis=1, tiled=True),
-        lax.all_gather(proj_weight, "row", axis=1, tiled=True),
-        lax.all_gather(up_weight, "row", axis=0, tiled=True),
-        lax.all_gather(down_weight, "row", axis=1, tiled=True),
-    )
     upstream = grad_out.astype(jnp.float32)
     grad_down_bias = jnp.sum(upstream, axis=0)
-    down_grads_full = spread_grads(grad_out)
+    down_grads_full = spread(grad_out)
     w_down_term = jnp.einsum(
-        "tf,td->fd", activated, down_grads_full, preferred_element_type=jnp.float32
-    )
-    grad_down_weight = lax.psum_scatter(w_down_term, "row", scatter_dimension=1, tiled=True)
+        "td,tf->df", down_grads_full, activated, preferred_element_type=jnp.float32
+    )
+    grad_down_weight = scatter_rows(w_down_term).T
     grad_activated = jnp.einsum(
-        "td,fd->tf", down_grads_full, down_back, preferred_element_type=jnp.float32
+        "td,df->tf", down_grads_full, down_full, preferred_element_type=jnp.float32
     )
     unused_value, gelu_pull = jax.vjp(
         lambda inner_value: jax.nn.gelu(inner_value, approximate=False), up_value
@@ -168,22 +200,22 @@
     grad_up = gelu_pull(grad_activated)[0].astype(jnp.bfloat16)
     grad_up_bias = jnp.sum(grad_up, axis=0, dtype=jnp.float32)
     w_up_term = jnp.einsum("td,tf->df", input_two, grad_up, preferred_element_type=jnp.float32)
-    grad_up_weight = lax.psum_scatter(w_up_term, "row", scatter_dimension=0, tiled=True)
-    grad_input_two = sum_grads(
-        jnp.einsum("tf,df->td", grad_up, up_back, preferred_element_type=jnp.float32)
+    grad_up_weight = scatter_rows(w_up_term)
+    grad_input_two = collect(
+        jnp.einsum("tf,df->td", grad_up, up_full, preferred_element_type=jnp.float32)
     )
     grad_gain_two = jnp.sum(grad_input_two * normed_two, axis=0)
     grad_shift_two = jnp.sum(grad_input_two, axis=0)
     grad_hidden = upstream + norm_backward(grad_input_two, normed_two, inverse_two, gain_two, D)
     grad_branch = grad_hidden.astype(jnp.bfloat16)
     grad_proj_bias = jnp.sum(grad_branch, axis=0, dtype=jnp.float32)
-    branch_grads_full = spread_grads(grad_branch)
+    branch_grads_full = spread(grad_branch)
     w_proj_term = jnp.einsum(
-        "te,td->ed", mixed_heads, branch_grads_full, preferred_element_type=jnp.float32
-    )
-    grad_proj_weight = lax.psum_scatter(w_proj_term, "row", scatter_dimension=1, tiled=True)
+        "td,te->de", branch_grads_full, mixed_heads, preferred_element_type=jnp.float32
+    )
+    grad_proj_weight = scatter_rows(w_proj_term).T
     grad_mixed = jnp.einsum(
-        "td,ed->te", branch_grads_full, proj_back, preferred_element_type=jnp.float32
+        "td,de->te", branch_grads_full, proj_full, preferred_element_type=jnp.float32
     ).astype(jnp.bfloat16)
     grad_query, grad_key, grad_value = lax.map(
         partial(attend_back, score_scale=score_scale),
@@ -195,30 +227,27 @@
             log_total,
         ),
     )
-    grad_stack = jnp.stack(
+    grad_stack = jnp.concatenate(
         [
             grad_query.reshape(row_count, local_width),
             grad_key.reshape(row_count, local_width),
             grad_value.reshape(row_count, local_width),
-        ]
+        ],
+        axis=1,
     ).astype(jnp.bfloat16)
-    grad_qv_bias = jnp.stack(
-        [
-            jnp.sum(grad_stack[0], axis=0, dtype=jnp.float32),
-            jnp.sum(grad_stack[2], axis=0, dtype=jnp.float32),
-        ]
-    )
+    stack_sums = jnp.sum(grad_stack, axis=0, dtype=jnp.float32)
+    grad_qv_bias = jnp.stack([stack_sums[:local_width], stack_sums[2 * local_width :]])
     w_qkv_term = jnp.einsum(
-        "td,jte->jde", input_one, grad_stack, preferred_element_type=jnp.float32
-    )
-    grad_qkv_weight = lax.psum_scatter(w_qkv_term, "row", scatter_dimension=1, tiled=True)
-    grad_input_one = sum_grads(
-        jnp.einsum("jte,jde->td", grad_stack, qkv_back, preferred_element_type=jnp.float32)
+        "td,te->de", input_one, grad_stack, preferred_element_type=jnp.float32
+    )
+    grad_qkv_weight = scatter_rows(w_qkv_term).reshape(-1, 3, local_width).swapaxes(0, 1)
+    grad_input_one = collect(
+        jnp.einsum("te,de->td", grad_stack, qkv_full, preferred_element_type=jnp.float32)
     )
     grad_gain_one = jnp.sum(grad_input_one * normed_one, axis=0)
     grad_shift_one = jnp.sum(grad_input_one, axis=0)
     grad_tokens = grad_hidden + norm_backward(grad_input_one, normed_one, inverse_one, gain_one, D)
-    small_sums = lax.psum(
+    small_sums = sum_small(
         (
             grad_gain_one,
             grad_shift_one,
@@ -228,8 +257,7 @@
             grad_shift_two,
             grad_up_bias,
             grad_down_bias,
-        ),
-        "row",
+        )
     )
     return (
         output,

time: 988 us -> 559 us (0.57)
  waiting for transfers between devices: 721 us -> 236 us
  starting transfers between devices: 1.07 us -> 31.4 us
  other arithmetic: 30.2 us -> 52.1 us
  matrix products: 102 us -> 86.4 us
  blocking collectives: 82.6 us -> 95.3 us
    reduce_scatter x7 -> x0, waiting for transfers between devices: 332 us -> none  [the longest x1 108 us: on_device(): lax.psum_scatter(w_up_term, 'row', scatter_dimension=0, tiled=True)]
    all_gather x8 -> x4, waiting for transfers between devices: 245 us -> 92.8 us  [gather_rows(): return lax.all_gather(block, 'row', axis=0, tiled=True)]
    unnamed x17 -> x4, waiting for transfers between devices: 144 us -> 1.91 us
    all_to_all x0 -> x5, waiting for transfers between devices: none -> 89.7 us  [the longest x4 87.5 us: scatter_rows(): got = lax.all_to_all(half, 'row', 0, 0, axis_index_groups=rings)]
    psum x1 -> x0, blocking collectives: 61.5 us -> none  [on_device(): lax.psum((grad_gain_one, grad_shift_one, grad_qv_bias, grad_proj_bias, gr...]
    ppermute x0 -> x8, waiting for transfers between devices: none -> 51.4 us  [the longest x4 30.8 us: collect(): got = lax.ppermute(block.astype(jnp.bfloat16), 'col', column_ring(shift))]
    all_gather x0 -> x1, blocking collectives: none -> 42.8 us  [sum_small(): flat = jnp.sum(lax.all_gather(flat, 'row', axis=0), axis=0)]
    reduce_sum x2 -> x10, other arithmetic: 0.36 us -> 25.8 us  [the longest x4 16.7 us: scatter_rows(): half = jnp.sum(got.astype(jnp.float32), axis=0).astype(jnp.bfloat16)]
  transfers between devices with their start and end apart: 16 -> 17, of which waited for: 15 -> 12; matrix products, arithmetic and copies ran while one was open for 8% -> 19% of each run, Pallas kernels for 0% -> 0%
where the time goes in v1:
time: 559 us; the launch traced here: 550 us
  waiting for transfers between devices  236 us (42%)
  blocking collectives  95.3 us (17%)
  matrix products  86.4 us (15%)
  other arithmetic  52.1 us (9%)
  local copies, waits for them, and re-layouts  33.8 us (6%)
  starting transfers between devices  31.4 us (6%)
  between operations  15 us (3%)
    all_gather x4, waiting for transfers between devices, gather_rows(): return lax.all_gather(block, 'row', axis=0, tiled=True)  92.8 us
    all_to_all x4, waiting for transfers between devices, scatter_rows(): got = lax.all_to_all(half, 'row', 0, 0, axis_index_groups=rings)  87.5 us
    all_gather x1, blocking collectives, sum_small(): flat = jnp.sum(lax.all_gather(flat, 'row', axis=0), axis=0)  42.8 us
    ppermute x4, waiting for transfers between devices, collect(): got = lax.ppermute(block.astype(jnp.bfloat16), 'col', column_ring(shift))  30.8 us
    psum x4, blocking collectives, row_totals(): lax.psum((jnp.sum(first_term, axis=1), jnp.sum(second_term, axis=1)), 'col')  28 us
    all_to_all x3, blocking collectives, scatter_rows(): lax.all_to_all(term.astype(jnp.bfloat16), 'row', 0, 0, axis_index_groups=...  24.5 us
    ppermute x4, waiting for transfers between devices, spread(): got = lax.ppermute(values, 'col', column_ring(shift))  20.6 us
    reduce_sum x4, other arithmetic, scatter_rows(): half = jnp.sum(got.astype(jnp.float32), axis=0).astype(jnp.bfloat16)  16.7 us
  transfers between devices with their start and end apart: 17, of which 12 were waited for; matrix products, arithmetic and copies ran while one was open for 19% of the time, Pallas kernels for 0%

profile of v1, /device:TPU:0, one launch (start us, length us, event | category | flops | bytes accessed | tf_op | source)
XLA Modules:
  0.0 549.7 jit_solution(1592557273672863549)
XLA Ops:
  12.3 6.0 %all-reduce.3 = (f32[577]{0:T(1024)S(1)}, f32[577]{0:T(1024)S(1)}) all-reduce(f32[577]{0:T(1024)S(1)} %get-tuple-element.140, f32[577]{0:T(1024)S(1)} %get-tuple-element.139), channel_id=1, replica_groups=mesh['row'=16,'col'=2] {'col'}, use_global_device_ids=true, to_apply=%region_3.0 | all-reduce | flops 1154 | bytes 9232 | tf_op jit(solution)/shard_map/psum | solution.py:17
  21.6 12.3 %collective-permute-done = bf16[577,512]{1,0:T(8,128)(2,1)S(1)} collective-permute-done((bf16[577,512]{1,0:T(8,128)(2,1)S(1)}, bf16[577,512]{1,0:T(8,128)(2,1)S(1)}, u32[]{:S(2)}, u32[]{:S(2)}) %collective-permute-start) | collective-permute-done | bytes 590880 | tf_op jit(solution)/shard_map/ppermute | solution.py:48
  34.1 25.0 %all-gather.6.cloned.1.call-done = bf16[1024,1536]{1,0:T(8,128)(2,1)} async-done(((bf16[64,1536]{1,0:T(8,128)(2,1)}), bf16[1024,1536]{1,0:T(8,128)(2,1)}) %all-gather.6.cloned.1.call-update) | async-done | bytes 3145744 | tf_op jit(solution)/shard_map/all_gather | solution.py:65
  59.1 3.9 fusion.44
  70.4 2.4 copy-done
  72.8 2.9 fusion.19
  75.7 21.8 %all-gather.8.cloned.1.call-done = bf16[1024,512]{1,0:T(8,128)(2,1)} async-done(((bf16[64,512]{1,0:T(8,128)(2,1)}), bf16[1024,512]{1,0:T(8,128)(2,1)}) %all-gather.8.cloned.1.call-update) | async-done | bytes 1048592 | tf_op jit(solution)/shard_map/all_gather | solution.py:65
  101.9 14.3 %collective-permute-done.1 = bf16[577,512]{1,0:T(8,128)(2,1)S(1)} collective-permute-done((bf16[577,512]{1,0:T(8,128)(2,1)S(1)}, bf16[577,512]{1,0:T(8,128)(2,1)S(1)}, u32[]{:S(2)}, u32[]{:S(2)}) %collective-permute-start.1) | collective-permute-done | bytes 590880 | tf_op jit(solution)/shard_map/ppermute | solution.py:59
  116.6 12.1 %all-reduce.2 = (f32[577]{0:T(1024)S(1)}, f32[577]{0:T(1024)S(1)}) all-reduce(f32[577]{0:T(1024)S(1)} %get-tuple-element.138, f32[577]{0:T(1024)S(1)} %get-tuple-element.137), channel_id=1, replica_groups=mesh['row'=16,'col'=2] {'col'}, use_global_device_ids=true, to_apply=%region_9.10 | all-reduce | flops 1154 | bytes 9232 | tf_op jit(solution)/shard_map/psum | solution.py:17
  137.6 8.3 %collective-permute-done.2 = bf16[577,512]{1,0:T(8,128)(2,1)S(1)} collective-permute-done((bf16[577,512]{1,0:T(8,128)(2,1)S(1)}, bf16[577,512]{1,0:T(8,128)(2,1)S(1)}, u32[]{:S(2)}, u32[]{:S(2)}) %collective-permute-start.2) | collective-permute-done | bytes 590880 | tf_op jit(solution)/shard_map/ppermute | solution.py:48
  149.0 7.3 %fusion.46 = f32[577,2048]{1,0:T(8,128)} fusion(bf16[577,1024]{1,0:T(8,128)(2,1)} %constant_dynamic-update-slice_fusion.12, bf16[1024,2048]{1,0:T(8,128)(2,1)} %all-gather.10.cloned.1.call-done), kind=kOutput, calls=%fused_computation.125 | convolution fusion | flops 2420113408 | bytes 10102784 | tf_op jit(solution)/shard_map/dot_general | solution.py:181
  156.4 43.6 %all-gather.12.cloned.1.call-done = bf16[1024,2048]{1,0:T(8,128)(2,1)} async-done(((bf16[64,2048]{1,0:T(8,128)(2,1)}), bf16[1024,2048]{1,0:T(8,128)(2,1)}) %all-gather.12.cloned.1.call-update) | async-done | bytes 4194320 | tf_op jit(solution)/shard_map/all_gather | solution.py:65
  200.0 15.8 %convert_reduce_fusion = (f32[2048]{0:T(1024)S(1)}, bf16[577,2048]{1,0:T(8,128)(2,1)S(1)}, f32[577,2048]{1,0:T(8,128)S(1)}) fusion(f32[577,2048]{1,0:T(8,128)} %fusion.46, f32[2048]{0:T(1024)S(1)} %copy-done.28, bf16[577,1024]{1,0:T(8,128)(2,1)} %constant_dynamic-update-slice_fusion.10, bf16[1024,2048]{1,0:T(8,128)(2,1)} %all-gather.12.cloned.1.call-done), kind=kOutput, calls=%fused_computation.14 | convolution fusion | flops 2508738560 | bytes 17209344 | tf_op jit(solution)/shard_map/td,df->tf/dot_general | solution.py:194
  218.0 2.7 fusion.47
  223.3 2.7 fusion.48
  226.7 5.0 convolution_convert_fusion.2
  231.7 2.4 copy.150
  234.0 16.4 %collective-permute-done.5 = bf16[577,512]{1,0:T(8,128)(2,1)S(1)} collective-permute-done((bf16[577,512]{1,0:T(8,128)(2,1)S(1)}, bf16[577,512]{1,0:T(8,128)(2,1)S(1)}, u32[]{:S(2)}, u32[]{:S(2)}) %collective-permute-start.5) | collective-permute-done | bytes 590880 | tf_op jit(solution)/shard_map/ppermute | solution.py:59
  252.0 5.0 all-reduce.1
  257.8 4.1 convert_reduce_fusion.7
  263.3 13.4 %convolution_convert_fusion.1 = bf16[1024,2048]{1,0:T(8,128)(2,1)S(1)} fusion(bf16[577,1024]{1,0:T(8,128)(2,1)} %constant_dynamic-update-slice_fusion.10, bf16[577,2048]{1,0:T(8,128)(2,1)S(1)} %copy-done.12), kind=kOutput, calls=%fused_computation.36 | convolution fusion | flops 2422210560 | bytes 7739392 | tf_op jit(solution)/shard_map/td,tf->df/dot_general | solution.py:190
  276.7 2.4 copy.149
  281.6 11.0 %multiply_reduce_fusion = (f32[8,577]{1,0:T(8,128)S(1)}, f32[8,577,577]{1,2,0:T(8,128)}) fusion(f32[8,577,577]{1,2,0:T(8,128)} %copy-done, f32[8,577]{1,0:T(8,128)S(1)} %log_add_fusion, bf16[577,8,64]{0,2,1:T(8,128)(2,1)S(1)} %bitcast.88, bf16[577,8,64]{0,2,1:T(8,128)(2,1)S(1)} %bitcast.100), kind=kOutput, calls=%fused_computation.1 | convolution fusion | flops 351568384 | bytes 22526080 | tf_op jit(solution)/shard_map/while/body/eval_jaxpr/qhe,khe->hqk/dot_general | solution.py:116
  293.3 6.2 %multiply_convert_fusion = bf16[8,577,577]{1,2,0:T(8,128)(2,1)S(1)} fusion(f32[8,577,577]{1,2,0:T(8,128)} %get-tuple-element.183, f32[8,577,577]{1,2,0:T(8,128)S(1)} %bitcast.82, f32[8,577]{1,0:T(8,128)S(1)} %get-tuple-element.182, f32[8,577]{1,0:T(8,128)S(1)} %log_add_fusion), kind=kLoop, calls=%fused_computation | loop fusion | flops 13317160 | bytes 26671248 | tf_op jit(solution)/shard_map/while/body/eval_jaxpr/convert_element_type | solution.py:121
  304.9 4.4 convolution_convert_fusion
  309.6 2.6 copy.132
  312.2 2.5 fusion.13
  314.8 5.4 all_to_all.40
  320.1 5.6 %all-to-all-start.4 = ((bf16[2,8,64,2048]{3,2,1,0:T(8,128)(2,1)}), bf16[2,8,64,2048]{3,2,1,0:T(8,128)(2,1)}, u32[]{:S(2)}, u32[]{:S(2)}) async-start(bf16[2,8,64,2048]{3,2,1,0:T(8,128)(2,1)} %bitcast.83), calls=%async_computation.4 | async-start | bytes 8388608 | tf_op jit(solution)/shard_map/all_to_all | solution.py:75
  325.8 2.4 reduce_sum.278
  330.2 11.9 %all_to_all.41 = bf16[2,8,64,2048]{3,2,1,0:T(8,128)(2,1)} all-to-all(bf16[2,8,64,2048]{3,2,1,0:T(8,128)(2,1)} %bitcast.84), channel_id=1, replica_groups={{0,2},{4,6},{8,10},{12,14},{16,18},{20,22},{24,26},{28,30},{1,3},{5,7},..., dimensions={0} | all-to-all | bytes 8388608 | tf_op jit(solution)/shard_map/all_to_all | solution.py:75
  342.1 7.3 %all_to_all.42 = bf16[2,8,64,1536]{3,2,1,0:T(8,128)(2,1)} all-to-all(bf16[2,8,64,1536]{3,2,1,0:T(8,128)(2,1)S(1)} %bitcast.85), channel_id=1, replica_groups={{0,2},{4,6},{8,10},{12,14},{16,18},{20,22},{24,26},{28,30},{1,3},{5,7},..., dimensions={0} | all-to-all | bytes 6291456 | tf_op jit(solution)/shard_map/all_to_all | solution.py:75
  349.4 3.5 all-to-all-start.3
  352.9 5.1 reduce_sum.280
  358.0 9.9 %all-to-all-done.3 = bf16[8,64,512]{2,1,0:T(8,128)(2,1)S(1)} async-done(((bf16[8,64,512]{2,1,0:T(8,128)(2,1)}), bf16[8,64,512]{2,1,0:T(8,128)(2,1)S(1)}, u32[]{:S(2)}, u32[]{:S(2)}) %all-to-all-start.3) | async-done | bytes 524320 | tf_op jit(solution)/shard_map/all_to_all | solution.py:77
  367.9 3.6 all-to-all-start.5
  371.5 5.2 reduce_sum.282
  376.7 43.2 %all-to-all-done.5 = bf16[8,64,2048]{2,1,0:T(8,128)(2,1)S(1)} async-done(((bf16[8,64,2048]{2,1,0:T(8,128)(2,1)}), bf16[8,64,2048]{2,1,0:T(8,128)(2,1)S(1)}, u32[]{:S(2)}, u32[]{:S(2)}) %all-to-all-start.5) | async-done | bytes 2097184 | tf_op jit(solution)/shard_map/all_to_all | solution.py:77
  419.9 4.4 all-to-all-start.7
  424.3 4.7 fusion.37
  433.6 4.1 reduce_sum.276
  437.8 34.4 %all-to-all-done.7 = bf16[8,64,2048]{2,1,0:T(8,128)(2,1)} async-done(((bf16[8,64,2048]{2,1,0:T(8,128)(2,1)}), bf16[8,64,2048]{2,1,0:T(8,128)(2,1)}, u32[]{:S(2)}, u32[]{:S(2)}) %all-to-all-start.7) | async-done | bytes 2097184 | tf_op jit(solution)/shard_map/all_to_all | solution.py:77
  472.1 4.3 all-to-all-start.1
  476.5 3.2 fusion.31
  479.7 42.8 %all-gather = f32[98304]{0:T(1024)} all-gather(f32[6144]{0:T(1024)S(1)} %constant_dynamic-update-slice_fusion), channel_id=2, replica_groups=mesh['row'=16,'col'=2] {'row'}, dimensions={0}, use_global_device_ids=true | all-gather | bytes 417792 | tf_op jit(solution)/shard_map/all_gather | solution.py:83
  526.6 5.0 all-reduce
  532.2 3.1 fusion.30
  537.1 2.8 convert_reduce_fusion.1
  (166 shorter events, 66.7 us)
Async XLA Ops:
  7.2 11.3 %copy-start.1 = (bf16[577,512]{1,0:T(8,128)(2,1)S(1)}, bf16[577,512]{1,0:T(8,128)(2,1)}, u32[]{:S(2)}) copy-start(bf16[577,512]{1,0:T(8,128)(2,1)} %param.14) | copy-start | bytes 1772548
  7.2 14.4 %copy-start.29 = (f32[2,512]{1,0:T(2,128)S(1)}, f32[2,512]{1,0:T(2,128)}, u32[]{:S(2)}) copy-start(f32[2,512]{1,0:T(2,128)} %param.18) | copy-start | bytes 12292
  7.2 51.9 %all-gather.6.cloned.1.call-start = ((), (), s32[]{:S(2)}) async-start(), calls=%async_computation.8 | async-start | bytes 3342336 | tf_op jit(solution)/shard_map/all_gather | solution.py:65
  8.9 88.5 %all-gather.8.cloned.1.call-start = ((), (), s32[]{:S(2)}) async-start(), calls=%async_computation.9 | async-start | bytes 1114112 | tf_op jit(solution)/shard_map/all_gather | solution.py:65
  9.7 139.3 %all-gather.10.cloned.1.call-start = ((), (), s32[]{:S(2)}) async-start(), calls=%async_computation.10 | async-start | bytes 4456448 | tf_op jit(solution)/shard_map/all_gather | solution.py:65
  10.4 189.5 %all-gather.12.cloned.1.call-start = ((), (), s32[]{:S(2)}) async-start(), calls=%async_computation.11 | async-start | bytes 4456448 | tf_op jit(solution)/shard_map/all_gather | solution.py:65
  19.5 14.5 %collective-permute-start = (bf16[577,512]{1,0:T(8,128)(2,1)S(1)}, bf16[577,512]{1,0:T(8,128)(2,1)S(1)}, u32[]{:S(2)}, u32[]{:S(2)}) collective-permute-start(bf16[577,512]{1,0:T(8,128)(2,1)S(1)} %get-tuple-element.161), channel_id=1, source_target_pairs={{0,1},{1,0},{2,3},{3,2},{4,5},{5,4},{6,7},{7,6},{8,9},{9,8},{10,11... | collective-permute-start | bytes 1772552 | tf_op jit(solution)/shard_map/ppermute | solution.py:48
  34.0 29.0 %copy-start.17 = (bf16[577,1024]{1,0:T(8,128)(2,1)}, bf16[577,1024]{1,0:T(8,128)(2,1)S(1)}, u32[]{:S(2)}) copy-start(bf16[577,1024]{1,0:T(8,128)(2,1)S(1)} %constant_dynamic-update-slice_fusion.14) | copy-start | bytes 3545092
  64.5 3.8 copy-start.3
  68.3 4.4 copy-start
  75.6 26.2 %copy-start.20 = (bf16[8,64,577]{2,1,0:T(8,128)(2,1)}, bf16[8,64,577]{2,1,0:T(8,128)(2,1)S(1)}, u32[]{:S(2)}) copy-start(bf16[8,64,577]{2,1,0:T(8,128)(2,1)S(1)} %fusion.19) | copy-start | bytes 1772548
  75.6 40.6 %copy-start.30 = (f32[512]{0:T(512)S(1)}, f32[512]{0:T(512)}, u32[]{:S(2)}) copy-start(f32[512]{0:T(512)} %param.20) | copy-start | bytes 6148
  99.6 30.3 %copy-start.26 = (f32[512]{0:T(512)S(1)}, f32[512]{0:T(512)}, u32[]{:S(2)}) copy-start(f32[512]{0:T(512)} %param.21) | copy-start | bytes 6148
  99.6 30.3 %copy-start.32 = (f32[512]{0:T(512)S(1)}, f32[512]{0:T(512)}, u32[]{:S(2)}) copy-start(f32[512]{0:T(512)} %param.22) | copy-start | bytes 6148
  99.8 16.4 %collective-permute-start.1 = (bf16[577,512]{1,0:T(8,128)(2,1)S(1)}, bf16[577,512]{1,0:T(8,128)(2,1)S(1)}, u32[]{:S(2)}, u32[]{:S(2)}) collective-permute-start(bf16[577,512]{1,0:T(8,128)(2,1)S(1)} %dynamic-slice_convert_fusion.3), channel_id=1, source_target_pairs={{0,1},{1,0},{2,3},{3,2},{4,5},{5,4},{6,7},{7,6},{8,9},{9,8},{10,11... | collective-permute-start | bytes 1772552 | tf_op jit(solution)/shard_map/ppermute | solution.py:59
  101.3 34.3 %collective-permute-start.4 = (bf16[577,512]{1,0:T(8,128)(2,1)}, bf16[577,512]{1,0:T(8,128)(2,1)}, u32[]{:S(2)}, u32[]{:S(2)}) collective-permute-start(bf16[577,512]{1,0:T(8,128)(2,1)} %param.27), channel_id=1, source_target_pairs={{0,1},{1,0},{2,3},{3,2},{4,5},{5,4},{6,7},{7,6},{8,9},{9,8},{10,11... | collective-permute-start | bytes 1772552 | tf_op jit(solution)/shard_map/ppermute | solution.py:48
  131.0 14.9 %collective-permute-start.2 = (bf16[577,512]{1,0:T(8,128)(2,1)S(1)}, bf16[577,512]{1,0:T(8,128)(2,1)S(1)}, u32[]{:S(2)}, u32[]{:S(2)}) collective-permute-start(bf16[577,512]{1,0:T(8,128)(2,1)S(1)} %get-tuple-element.158), channel_id=1, source_target_pairs={{0,1},{1,0},{2,3},{3,2},{4,5},{5,4},{6,7},{7,6},{8,9},{9,8},{10,11... | collective-permute-start | bytes 1772552 | tf_op jit(solution)/shard_map/ppermute | solution.py:48
  146.7 53.3 %copy-start.28 = (f32[2048]{0:T(1024)S(1)}, f32[2048]{0:T(1024)}, u32[]{:S(2)}) copy-start(f32[2048]{0:T(1024)} %param.24) | copy-start | bytes 24580
  200.0 15.9 %copy-start.7 = (f32[577,2048]{1,0:T(8,128)S(1)}, f32[577,2048]{1,0:T(8,128)}, u32[]{:S(2)}) copy-start(f32[577,2048]{1,0:T(8,128)} %fusion.46) | copy-start | bytes 14180356
  215.8 2.2 copy-start.34
  218.0 2.7 copy-start.11
  218.0 5.2 copy-start.33
  220.7 5.2 copy-start.15
  221.8 35.2 %collective-permute-start.3 = (bf16[577,512]{1,0:T(8,128)(2,1)}, bf16[577,512]{1,0:T(8,128)(2,1)S(1)}, u32[]{:S(2)}, u32[]{:S(2)}) collective-permute-start(bf16[577,512]{1,0:T(8,128)(2,1)} %dynamic-slice_convert_fusion.2), channel_id=1, source_target_pairs={{0,1},{1,0},{2,3},{3,2},{4,5},{5,4},{6,7},{7,6},{8,9},{9,8},{10,11... | collective-permute-start | bytes 1772552 | tf_op jit(solution)/shard_map/ppermute | solution.py:59
  226.1 24.4 %collective-permute-start.5 = (bf16[577,512]{1,0:T(8,128)(2,1)S(1)}, bf16[577,512]{1,0:T(8,128)(2,1)S(1)}, u32[]{:S(2)}, u32[]{:S(2)}) collective-permute-start(bf16[577,512]{1,0:T(8,128)(2,1)S(1)} %dynamic-slice_convert_fusion.1), channel_id=1, source_target_pairs={{0,1},{1,0},{2,3},{3,2},{4,5},{5,4},{6,7},{7,6},{8,9},{9,8},{10,11... | collective-permute-start | bytes 1772552 | tf_op jit(solution)/shard_map/ppermute | solution.py:59
  234.0 23.7 %copy-start.31 = (f32[512]{0:T(512)S(1)}, f32[512]{0:T(512)}, u32[]{:S(2)}) copy-start(f32[512]{0:T(512)} %param.26) | copy-start | bytes 6148
  257.8 5.6 %copy-start.12 = (bf16[577,2048]{1,0:T(8,128)(2,1)S(1)}, bf16[577,2048]{1,0:T(8,128)(2,1)}, u32[]{:S(2)}) copy-start(bf16[577,2048]{1,0:T(8,128)(2,1)} %copy-done.11) | copy-start | bytes 7090180
  261.8 17.5 %collective-permute-start.6 = (bf16[577,512]{1,0:T(8,128)(2,1)S(1)}, bf16[577,512]{1,0:T(8,128)(2,1)S(1)}, u32[]{:S(2)}, u32[]{:S(2)}) collective-permute-start(bf16[577,512]{1,0:T(8,128)(2,1)S(1)} %get-tuple-element.153), channel_id=1, source_target_pairs={{0,1},{1,0},{2,3},{3,2},{4,5},{5,4},{6,7},{7,6},{8,9},{9,8},{10,11... | collective-permute-start | bytes 1772552 | tf_op jit(solution)/shard_map/ppermute | solution.py:48
  281.6 11.0 %slice-start = ((s8[11960320]{0:T(1024)(128)(4,1)}), s8[4194304]{0:T(1024)(128)(4,1)S(1)}, s32[]{:S(2)}) async-start(s8[11960320]{0:T(1024)(128)(4,1)} %bitcast.81), calls=%async_computation.12 | async-start | bytes 8388608
  281.6 11.0 %slice-start.1 = ((s8[11960320]{0:T(1024)(128)(4,1)}), s8[4194304]{0:T(1024)(128)(4,1)S(1)}, s32[]{:S(2)}) async-start(s8[11960320]{0:T(1024)(128)(4,1)} %bitcast.81), calls=%async_computation.13 | async-start | bytes 8388608
  281.6 11.7 %slice-start.2 = ((s8[11960320]{0:T(1024)(128)(4,1)}), s8[3571712]{0:T(1024)(128)(4,1)S(1)}, s32[]{:S(2)}) async-start(s8[11960320]{0:T(1024)(128)(4,1)} %bitcast.81), calls=%async_computation.14 | async-start | bytes 7143424
  300.8 4.1 copy-start.5
  302.7 2.2 copy-start.10
  302.7 2.2 copy-start.18
  304.8 4.4 copy-start.9
  320.1 10.1 %all-to-all-start.4 = ((bf16[2,8,64,2048]{3,2,1,0:T(8,128)(2,1)}), bf16[2,8,64,2048]{3,2,1,0:T(8,128)(2,1)}, u32[]{:S(2)}, u32[]{:S(2)}) async-start(bf16[2,8,64,2048]{3,2,1,0:T(8,128)(2,1)} %bitcast.83), calls=%async_computation.4 | async-start | bytes 8388608 | tf_op jit(solution)/shard_map/all_to_all | solution.py:75
  349.4 18.5 %all-to-all-start.3 = ((bf16[8,64,512]{2,1,0:T(8,128)(2,1)}), bf16[8,64,512]{2,1,0:T(8,128)(2,1)S(1)}, u32[]{:S(2)}, u32[]{:S(2)}) async-start(bf16[8,64,512]{2,1,0:T(8,128)(2,1)} %reduce_sum.278), calls=%async_computation.3 | async-start | bytes 1048576 | tf_op jit(solution)/shard_map/all_to_all | solution.py:77
  367.9 8.8 %copy-start.13 = (bf16[8,64,512]{2,1,0:T(8,128)(2,1)}, bf16[8,64,512]{2,1,0:T(8,128)(2,1)S(1)}, u32[]{:S(2)}) copy-start(bf16[8,64,512]{2,1,0:T(8,128)(2,1)S(1)} %all-to-all-done.3) | copy-start | bytes 1572868
  367.9 52.1 %all-to-all-start.5 = ((bf16[8,64,2048]{2,1,0:T(8,128)(2,1)}), bf16[8,64,2048]{2,1,0:T(8,128)(2,1)S(1)}, u32[]{:S(2)}, u32[]{:S(2)}) async-start(bf16[8,64,2048]{2,1,0:T(8,128)(2,1)} %reduce_sum.280), calls=%async_computation.5 | async-start | bytes 4194304 | tf_op jit(solution)/shard_map/all_to_all | solution.py:77
  376.7 47.6 %copy-start.6 = (bf16[8,64,577]{2,1,0:T(8,128)(2,1)S(1)}, bf16[8,64,577]{2,1,0:T(8,128)(2,1)}, u32[]{:S(2)}) copy-start(bf16[8,64,577]{2,1,0:T(8,128)(2,1)} %copy-done.5) | copy-start | bytes 1772548
  419.9 52.2 %all-to-all-start.7 = ((bf16[8,64,2048]{2,1,0:T(8,128)(2,1)}), bf16[8,64,2048]{2,1,0:T(8,128)(2,1)}, u32[]{:S(2)}, u32[]{:S(2)}) async-start(bf16[8,64,2048]{2,1,0:T(8,128)(2,1)} %reduce_sum.282), calls=%async_computation.7 | async-start | bytes 4194304 | tf_op jit(solution)/shard_map/all_to_all | solution.py:77
  431.3 45.1 %collective-permute-start.7 = (bf16[577,512]{1,0:T(8,128)(2,1)}, bf16[577,512]{1,0:T(8,128)(2,1)}, u32[]{:S(2)}, u32[]{:S(2)}) collective-permute-start(bf16[577,512]{1,0:T(8,128)(2,1)} %dynamic-slice_convert_fusion), channel_id=1, source_target_pairs={{0,1},{1,0},{2,3},{3,2},{4,5},{5,4},{6,7},{7,6},{8,9},{9,8},{10,11... | collective-permute-start | bytes 1772552 | tf_op jit(solution)/shard_map/ppermute | solution.py:59
  433.6 42.9 %copy-start.2 = (bf16[577,512]{1,0:T(8,128)(2,1)S(1)}, bf16[577,512]{1,0:T(8,128)(2,1)}, u32[]{:S(2)}) copy-start(bf16[577,512]{1,0:T(8,128)(2,1)} %param.14) | copy-start | bytes 1772548
  433.6 42.9 %copy-start.23 = (f32[577]{0:T(1024)S(1)}, f32[577]{0:T(1024)}, u32[]{:S(2)}) copy-start(f32[577]{0:T(1024)} %copy-done.22) | copy-start | bytes 6928
  433.6 42.9 %copy-start.25 = (f32[577]{0:T(1024)S(1)}, f32[577]{0:T(1024)}, u32[]{:S(2)}) copy-start(f32[577]{0:T(1024)} %copy-done.24) | copy-start | bytes 6928
  433.6 42.9 %copy-start.27 = (f32[512]{0:T(512)S(1)}, f32[512]{0:T(512)}, u32[]{:S(2)}) copy-start(f32[512]{0:T(512)} %param.15) | copy-start | bytes 6148
  472.1 67.8 %all-to-all-start.1 = ((bf16[8,64,1536]{2,1,0:T(8,128)(2,1)}), bf16[8,64,1536]{2,1,0:T(8,128)(2,1)}, u32[]{:S(2)}, u32[]{:S(2)}) async-start(bf16[8,64,1536]{2,1,0:T(8,128)(2,1)} %reduce_sum.276), calls=%async_computation.1 | async-start | bytes 3145728 | tf_op jit(solution)/shard_map/all_to_all | solution.py:77
  479.7 55.6 %copy-start.14 = (bf16[8,64,512]{2,1,0:T(8,128)(2,1)S(1)}, bf16[8,64,512]{2,1,0:T(8,128)(2,1)}, u32[]{:S(2)}) copy-start(bf16[8,64,512]{2,1,0:T(8,128)(2,1)} %copy-done.13) | copy-start | bytes 1572868
  (7 other events, 8.3 us)
Sparse Core Ops, SparseCore 0:
  10.9 48.1 all-gather.5
  61.2 36.1 all-gather.7
  99.6 49.3 all-gather.9
  151.0 48.8 all-gather.11

commit v2 on v1

--- a/solution.py
+++ b/solution.py
@@ -14,7 +14,11 @@
 
 
 def row_totals(first_term, second_term):
-    return lax.psum((jnp.sum(first_term, axis=1), jnp.sum(second_term, axis=1)), "col")
+    sums = jnp.stack([jnp.sum(first_term, axis=1), jnp.sum(second_term, axis=1)])
+    total = sums
+    for shift in range(1, lax.axis_size("col")):
+        total = total + lax.ppermute(sums, "col", column_ring(shift))
+    return total[0], total[1]
 
 
 def norm_forward(values, gain_value, shift_value, feature_width):
@@ -65,22 +69,29 @@
     return lax.all_gather(block, "row", axis=0, tiled=True)
 
 
-def scatter_rows(term):
+def halve(term):
+    count, core = lax.axis_size("row"), lax.axis_index("row") % 2
+    rows, width = term.shape
+    term = term.reshape(count // 2, 2, rows // count, width)
+    mine = lax.dynamic_index_in_dim(term, core, 1, keepdims=False)
+    other = lax.dynamic_index_in_dim(term, 1 - core, 1, keepdims=False)
+    got = lax.ppermute(other.astype(jnp.bfloat16), "row", [(i, i ^ 1) for i in range(count)])
+    return (mine + got.astype(jnp.float32)).astype(jnp.bfloat16)
+
+
+def scatter_rows(half):
     count = lax.axis_size("row")
-    chips = count // 2
-    pairs = [[i, i + 1] for i in range(0, count, 2)]
     rings = [list(range(0, count, 2)), list(range(1, count, 2))]
-    rows, width = term.shape
-    term = term.reshape(chips, 2, rows // count, width).swapaxes(0, 1)
-    got = lax.all_to_all(term.astype(jnp.bfloat16), "row", 0, 0, axis_index_groups=pairs)
-    half = jnp.sum(got.astype(jnp.float32), axis=0).astype(jnp.bfloat16)
     got = lax.all_to_all(half, "row", 0, 0, axis_index_groups=rings)
     return jnp.sum(got.astype(jnp.float32), axis=0)
 
 
 def sum_small(parts):
     flat = jnp.concatenate([part.reshape(-1) for part in parts])
-    flat = jnp.sum(lax.all_gather(flat, "row", axis=0), axis=0)
+    count, step = lax.axis_size("row"), 1
+    while step < count:
+        flat = flat + lax.ppermute(flat, "row", [(i, i ^ step) for i in range(count)])
+        step *= 2
     outs, start = [], 0
     for part in parts:
         outs.append(flat[start : start + part.size].reshape(part.shape))
@@ -153,12 +164,15 @@
     def to_images(values):
         return values.reshape(image_count, SEQ, head_count, HD)
 
-    qkv_full, proj_full, up_full, down_full = (
-        gather_rows(qkv_weight.swapaxes(0, 1).reshape(-1, 3 * local_width)),
-        gather_rows(proj_weight.T),
-        gather_rows(up_weight),
-        gather_rows(down_weight.T),
-    )
+    hidden_width = up_weight.shape[1]
+    first_full = gather_rows(
+        jnp.concatenate(
+            [qkv_weight[0], qkv_weight[1], qkv_weight[2], proj_weight.T], axis=1
+        )
+    )
+    second_full = gather_rows(jnp.concatenate([up_weight, down_weight.T], axis=1))
+    qkv_full, proj_full = first_full[:, : 3 * local_width], first_full[:, 3 * local_width :]
+    up_full, down_full = second_full[:, :hidden_width], second_full[:, hidden_width:]
     x_value = tokens.astype(jnp.float32)
     normed_one, inverse_one, pre_one = norm_forward(x_value, gain_one, shift_one, D)
     input_one = spread(pre_one.astype(jnp.bfloat16))
@@ -190,7 +204,7 @@
     w_down_term = jnp.einsum(
         "td,tf->df", down_grads_full, activated, preferred_element_type=jnp.float32
     )
-    grad_down_weight = scatter_rows(w_down_term).T
+    down_half = halve(w_down_term)
     grad_activated = jnp.einsum(
         "td,df->tf", down_grads_full, down_full, preferred_element_type=jnp.float32
     )
@@ -198,9 +212,11 @@
         lambda inner_value: jax.nn.gelu(inner_value, approximate=False), up_value
     )
     grad_up = gelu_pull(grad_activated)[0].astype(jnp.bfloat16)
+    down_half, grad_up = lax.optimization_barrier((down_half, grad_up))
+    grad_down_weight = scatter_rows(down_half).T
     grad_up_bias = jnp.sum(grad_up, axis=0, dtype=jnp.float32)
     w_up_term = jnp.einsum("td,tf->df", input_two, grad_up, preferred_element_type=jnp.float32)
-    grad_up_weight = scatter_rows(w_up_term)
+    up_half = halve(w_up_term)
     grad_input_two = collect(
         jnp.einsum("tf,df->td", grad_up, up_full, preferred_element_type=jnp.float32)
     )
@@ -208,15 +224,19 @@
     grad_shift_two = jnp.sum(grad_input_two, axis=0)
     grad_hidden = upstream + norm_backward(grad_input_two, normed_two, inverse_two, gain_two, D)
     grad_branch = grad_hidden.astype(jnp.bfloat16)
+    up_half, grad_branch = lax.optimization_barrier((up_half, grad_branch))
+    grad_up_weight = scatter_rows(up_half)
     grad_proj_bias = jnp.sum(grad_branch, axis=0, dtype=jnp.float32)
     branch_grads_full = spread(grad_branch)
     w_proj_term = jnp.einsum(
         "td,te->de", branch_grads_full, mixed_heads, preferred_element_type=jnp.float32
     )
-    grad_proj_weight = scatter_rows(w_proj_term).T
+    proj_half = halve(w_proj_term)
     grad_mixed = jnp.einsum(
         "td,de->te", branch_grads_full, proj_full, preferred_element_type=jnp.float32
     ).astype(jnp.bfloat16)
+    proj_half, grad_mixed = lax.optimization_barrier((proj_half, grad_mixed))
+    grad_proj_weight = scatter_rows(proj_half).T
     grad_query, grad_key, grad_value = lax.map(
         partial(attend_back, score_scale=score_scale),
         (
@@ -240,7 +260,7 @@
     w_qkv_term = jnp.einsum(
         "td,te->de", input_one, grad_stack, preferred_element_type=jnp.float32
     )
-    grad_qkv_weight = scatter_rows(w_qkv_term).reshape(-1, 3, local_width).swapaxes(0, 1)
+    grad_qkv_weight = scatter_rows(halve(w_qkv_term)).reshape(-1, 3, local_width).swapaxes(0, 1)
     grad_input_one = collect(
         jnp.einsum("te,de->td", grad_stack, qkv_full, preferred_element_type=jnp.float32)
     )

time: 559 us -> 402 us (0.72)
  blocking collectives: 95.3 us -> 0 us
  waiting for transfers between devices: 236 us -> 157 us
  starting transfers between devices: 31.4 us -> 43 us
    all_to_all x4, waiting for transfers between devices: 87.5 us -> 19.4 us  [scatter_rows(): got = lax.all_to_all(half, 'row', 0, 0, axis_index_groups=rings)]
    all_gather x4 -> x2, waiting for transfers between devices: 92.8 us -> 40.6 us  [gather_rows(): return lax.all_gather(block, 'row', axis=0, tiled=True)]
    all_gather x1 -> x0, blocking collectives: 42.8 us -> none  [sum_small(): flat = jnp.sum(lax.all_gather(flat, 'row', axis=0), axis=0)]
    ppermute x0 -> x12, waiting for transfers between devices: none -> 30.3 us  [the longest x4 22.3 us: sum_small(): lax.ppermute(flat, 'row', [(i, i ^ step) for i in range(count)])]
    psum x4 -> x0, blocking collectives: 28 us -> none  [row_totals(): lax.psum((jnp.sum(first_term, axis=1), jnp.sum(second_term, axis=1)), 'col')]
    all_to_all x3 -> x0, blocking collectives: 24.5 us -> none  [scatter_rows(): lax.all_to_all(term.astype(jnp.bfloat16), 'row', 0, 0, axis_index_groups=...]
    ppermute x4, waiting for transfers between devices: 20.6 us -> 41.8 us  [spread(): got = lax.ppermute(values, 'col', column_ring(shift))]
    convert_element_type x1 -> x5, other arithmetic: 1.2 us -> 17.6 us  [the longest x4 13.7 us: halve(): return (mine + got.astype(jnp.float32)).astype(jnp.bfloat16)]
  transfers between devices with their start and end apart: 17 -> 26, of which waited for: 12 -> 16; matrix products, arithmetic and copies ran while one was open for 19% -> 32% of each run, Pallas kernels for 0% -> 0%
where the time goes in v2:
time: 402 us; the launch traced here: 395 us
  waiting for transfers between devices  157 us (39%)
  matrix products  91 us (23%)
  other arithmetic  50.2 us (12%)
  starting transfers between devices  43 us (11%)
  local copies, waits for them, and re-layouts  38.9 us (10%)
  between operations  15.2 us (4%)
    ppermute x4, waiting for transfers between devices, spread(): got = lax.ppermute(values, 'col', column_ring(shift))  41.8 us
    all_gather x2, waiting for transfers between devices, gather_rows(): return lax.all_gather(block, 'row', axis=0, tiled=True)  40.6 us
    ppermute x4, waiting for transfers between devices, collect(): got = lax.ppermute(block.astype(jnp.bfloat16), 'col', column_ring(shift))  24.8 us
    ppermute x4, waiting for transfers between devices, sum_small(): lax.ppermute(flat, 'row', [(i, i ^ step) for i in range(count)])  22.3 us
    all_to_all x4, waiting for transfers between devices, scatter_rows(): got = lax.all_to_all(half, 'row', 0, 0, axis_index_groups=rings)  19.4 us
    all_to_all x4, starting transfers between devices, scatter_rows(): got = lax.all_to_all(half, 'row', 0, 0, axis_index_groups=rings)  16.4 us
    dot_general x1, matrix products, on_device(): jnp.dot(input_two, up_full, preferred_element_type=jnp.float32) + up_bias  16 us
    unnamed x91, local copies, waits for them, and re-layouts  15.3 us
  transfers between devices with their start and end apart: 26, of which 16 were waited for; matrix products, arithmetic and copies ran while one was open for 32% of the time, Pallas kernels for 0%

profile of v2, /device:TPU:0, one launch (start us, length us, event | category | flops | bytes accessed | tf_op | source)
XLA Modules:
  0.0 395.3 jit_solution(11633048786092891006)
XLA Ops:
  12.1 3.1 collective-permute-start
  19.4 12.3 %collective-permute-done.1 = bf16[577,512]{1,0:T(8,128)(2,1)S(1)} collective-permute-done((bf16[577,512]{1,0:T(8,128)(2,1)S(1)}, bf16[577,512]{1,0:T(8,128)(2,1)S(1)}, u32[]{:S(2)}, u32[]{:S(2)}) %collective-permute-start.1) | collective-permute-done | bytes 590880 | tf_op jit(solution)/shard_map/ppermute | solution.py:52
  31.9 32.0 %all-gather.3.cloned.1.call-done = bf16[1024,2048]{1,0:T(8,128)(2,1)} async-done(((bf16[64,2048]{1,0:T(8,128)(2,1)}), bf16[1024,2048]{1,0:T(8,128)(2,1)}) %all-gather.3.cloned.1.call-update) | async-done | bytes 4194320 | tf_op jit(solution)/shard_map/all_gather | solution.py:69
  63.9 3.9 fusion.26
  75.2 2.3 copy-done
  77.5 3.4 fusion.38
  80.9 2.4 fusion.56
  85.0 14.2 %collective-permute-done.2 = bf16[577,512]{1,0:T(8,128)(2,1)S(1)} collective-permute-done((bf16[577,512]{1,0:T(8,128)(2,1)S(1)}, bf16[577,512]{1,0:T(8,128)(2,1)S(1)}, u32[]{:S(2)}, u32[]{:S(2)}) %collective-permute-start.2) | collective-permute-done | bytes 590880 | tf_op jit(solution)/shard_map/ppermute | solution.py:63
  110.6 7.3 %collective-permute-done.6 = bf16[577,512]{1,0:T(8,128)(2,1)} collective-permute-done((bf16[577,512]{1,0:T(8,128)(2,1)}, bf16[577,512]{1,0:T(8,128)(2,1)}, u32[]{:S(2)}, u32[]{:S(2)}) %collective-permute-start.6) | collective-permute-done | bytes 590880 | tf_op jit(solution)/shard_map/ppermute | solution.py:52
  119.9 9.0 %collective-permute-done.4 = bf16[577,512]{1,0:T(8,128)(2,1)} collective-permute-done((bf16[577,512]{1,0:T(8,128)(2,1)}, bf16[577,512]{1,0:T(8,128)(2,1)}, u32[]{:S(2)}, u32[]{:S(2)}) %collective-permute-start.4) | collective-permute-done | bytes 590880 | tf_op jit(solution)/shard_map/ppermute | solution.py:52
  130.9 8.6 %all-gather.5.cloned.1.call-done = bf16[1024,4096]{1,0:T(8,128)(2,1)} async-done(((bf16[64,4096]{1,0:T(8,128)(2,1)}), bf16[1024,4096]{1,0:T(8,128)(2,1)}) %all-gather.5.cloned.1.call-update) | async-done | bytes 8388624 | tf_op jit(solution)/shard_map/all_gather | solution.py:69
  139.5 16.0 %multiply_convert_fusion.1 = (bf16[577,2048]{1,0:T(8,128)(2,1)S(1)}, f32[577,2048]{1,0:T(8,128)}, f32[577,2048]{1,0:T(8,128)}) fusion(f32[2048]{0:T(1024)S(1)} %copy-done.34, bf16[577,1024]{1,0:T(8,128)(2,1)} %constant_dynamic-update-slice_fusion.4, bf16[1024,4096]{1,0:T(8,128)(2,1)} %all-gather.5.cloned.1.call-done), kind=kOutput, calls=%fused_computation.16 | convolution fusion | flops 2498105344 | bytes 17215488 | tf_op jit(solution)/shard_map/dot_general | solution.py:195
  155.5 5.7 %fusion.81 = f32[1024,2048]{1,0:T(8,128)S(1)} fusion(bf16[577,1024]{1,0:T(8,128)(2,1)} %constant_dynamic-update-slice_fusion.2, bf16[577,2048]{1,0:T(8,128)(2,1)S(1)} %get-tuple-element.137), kind=kOutput, calls=%fused_computation.170 | convolution fusion | flops 2420113408 | bytes 11933696 | tf_op jit(solution)/shard_map/td,tf->df/dot_general | solution.py:204
  161.2 3.3 copy-done.8
  166.4 9.5 %add_convert_fusion = bf16[577,2048]{1,0:T(8,128)(2,1)S(1)} fusion(f32[577,2048]{1,0:T(8,128)} %get-tuple-element.138, f32[577,2048]{1,0:T(8,128)} %get-tuple-element.163, f32[2048]{0:T(1024)S(1)} %copy-done.34, bf16[577,1024]{1,0:T(8,128)(2,1)} %constant_dynamic-update-slice_fusion.2, bf16[1024,4096]{1,0:T(8,128)(2,1)} %all-gather.5.cloned.1.call-done), kind=kOutput, calls=%fused_computation.15 | convolution fusion | flops 2437838848 | bytes 17330176 | tf_op jit(solution)/shard_map/td,df->tf/dot_general | solution.py:208
  175.9 4.6 %fusion.14 = bf16[8,64,2048]{2,1,0:T(8,128)(2,1)} fusion(bf16[8,64,2048]{2,1,0:T(8,128)(2,1)} %collective-permute-done.7, f32[8,2,64,2048]{3,2,1,0:T(8,128)S(1)} %bitcast.103, s32[]{:T(128)S(6)} %select_n.76), kind=kLoop, calls=%fused_computation.33 | loop fusion | flops 3145728 | bytes 8388612 | tf_op jit(solution)/shard_map/convert_element_type | solution.py:79
  180.5 4.9 %fusion.82 = f32[1024,2048]{1,0:T(8,128)S(1)} fusion(bf16[577,1024]{1,0:T(8,128)(2,1)} %constant_dynamic-update-slice_fusion.4, bf16[577,2048]{1,0:T(8,128)(2,1)S(1)} %add_convert_fusion), kind=kOutput, calls=%fused_computation.171 | convolution fusion | flops 2420113408 | bytes 11933696 | tf_op jit(solution)/shard_map/td,tf->df/dot_general | solution.py:218
  185.5 3.3 copy-done.7
  190.7 2.9 fusion.19
  195.3 2.7 fusion.17
  199.5 10.6 %collective-permute-done.8 = bf16[577,512]{1,0:T(8,128)(2,1)S(1)} collective-permute-done((bf16[577,512]{1,0:T(8,128)(2,1)S(1)}, bf16[577,512]{1,0:T(8,128)(2,1)S(1)}, u32[]{:S(2)}, u32[]{:S(2)}) %collective-permute-start.8) | collective-permute-done | bytes 590880 | tf_op jit(solution)/shard_map/ppermute | solution.py:63
  213.3 4.4 %all-to-all-start.3 = ((bf16[8,64,2048]{2,1,0:T(8,128)(2,1)}), bf16[8,64,2048]{2,1,0:T(8,128)(2,1)}, u32[]{:S(2)}, u32[]{:S(2)}) async-start(bf16[8,64,2048]{2,1,0:T(8,128)(2,1)} %fusion.14), calls=%async_computation.3 | async-start | bytes 4194304 | tf_op jit(solution)/shard_map/all_to_all | solution.py:85
  217.6 4.8 %collective-permute-done.9 = f32[2,577]{1,0:T(2,128)S(1)} collective-permute-done((f32[2,577]{1,0:T(2,128)S(1)}, f32[2,577]{1,0:T(2,128)S(1)}, u32[]{:S(2)}, u32[]{:S(2)}) %collective-permute-start.9) | collective-permute-done | bytes 4648 | tf_op jit(solution)/shard_map/ppermute | solution.py:20
  222.5 3.9 fusion.75
  226.4 5.1 %fusion.13 = bf16[8,64,2048]{2,1,0:T(8,128)(2,1)} fusion(bf16[8,64,2048]{2,1,0:T(8,128)(2,1)} %collective-permute-done.10, f32[8,2,64,2048]{3,2,1,0:T(8,128)} %bitcast.101, s32[]{:T(128)S(6)} %select_n.76), kind=kLoop, calls=%fused_computation.31 | loop fusion | flops 3145728 | bytes 8388612 | tf_op jit(solution)/shard_map/convert_element_type | solution.py:79
  233.2 13.1 %collective-permute-done.11 = bf16[577,512]{1,0:T(8,128)(2,1)S(1)} collective-permute-done((bf16[577,512]{1,0:T(8,128)(2,1)S(1)}, bf16[577,512]{1,0:T(8,128)(2,1)S(1)}, u32[]{:S(2)}, u32[]{:S(2)}) %collective-permute-start.11) | collective-permute-done | bytes 590880 | tf_op jit(solution)/shard_map/ppermute | solution.py:52
  247.8 2.5 fusion.83
  250.5 2.8 convolution_convert_fusion
  255.7 11.7 %multiply_reduce_fusion = (f32[8,577]{1,0:T(8,128)S(1)}, f32[8,577,577]{1,2,0:T(8,128)}) fusion(f32[8,577,577]{1,2,0:T(8,128)} %copy-done, f32[8,577]{1,0:T(8,128)S(1)} %log_add_fusion, bf16[577,8,64]{0,2,1:T(8,128)(2,1)S(1)} %bitcast.91, bf16[577,8,64]{0,2,1:T(8,128)(2,1)} %bitcast.109), kind=kOutput, calls=%fused_computation.1 | convolution fusion | flops 351568384 | bytes 22526080 | tf_op jit(solution)/shard_map/while/body/eval_jaxpr/qhe,khe->hqk/dot_general | solution.py:127
  267.5 3.9 all-to-all-start.1
  271.4 9.1 %multiply_convert_fusion = bf16[8,577,577]{1,2,0:T(8,128)(2,1)S(1)} fusion(f32[8,577,577]{1,2,0:T(8,128)} %get-tuple-element.165, f32[8,577,577]{1,2,0:T(8,128)} %copy-done, f32[8,577]{1,0:T(8,128)S(1)} %get-tuple-element.164, f32[8,577]{1,0:T(8,128)S(1)} %log_add_fusion), kind=kLoop, calls=%fused_computation | loop fusion | flops 13317160 | bytes 26671248 | tf_op jit(solution)/shard_map/while/body/eval_jaxpr/convert_element_type | solution.py:132
  280.5 2.5 copy-done.1
  286.7 4.4 %all-to-all-start.2 = ((bf16[8,64,2048]{2,1,0:T(8,128)(2,1)}), bf16[8,64,2048]{2,1,0:T(8,128)(2,1)}, u32[]{:S(2)}, u32[]{:S(2)}) async-start(bf16[8,64,2048]{2,1,0:T(8,128)(2,1)} %fusion.13), calls=%async_computation.2 | async-start | bytes 4194304 | tf_op jit(solution)/shard_map/all_to_all | solution.py:85
  291.1 4.6 %fusion.34 = bf16[8,64,577]{2,1,0:T(8,128)(2,1)S(1)} fusion(bf16[577,8,64]{0,2,1:T(8,128)(2,1)S(1)} %bitcast.94, bf16[8,577,577]{1,2,0:T(8,128)(2,1)} %copy-done.1), kind=kOutput, calls=%fused_computation.68 | convolution fusion | flops 341510144 | bytes 6508560 | tf_op jit(solution)/shard_map/while/body/eval_jaxpr/hqk,qhe->khe/dot_general | solution.py:136
  295.7 6.8 %fusion.35 = bf16[8,64,577]{2,1,0:T(8,128)(2,1)S(1)} fusion(bf16[577,8,64]{0,2,1:T(8,128)(2,1)S(1)} %bitcast.92, f32[8,577,577]{1,2,0:T(8,128)} %copy-done, f32[8,577]{1,0:T(8,128)S(1)} %log_add_fusion), kind=kOutput, calls=%fused_computation.69 | convolution fusion | flops 349205024 | bytes 11853888 | tf_op jit(solution)/shard_map/while/body/eval_jaxpr/hqk,qhe->khe/dot_general | solution.py:124
  302.5 2.7 fusion.73
  305.3 2.6 copy-done.10
  311.5 4.4 %fusion.24 = f32[577,1024]{1,0:T(8,128)S(1)} fusion(bf16[1024,2048]{1,0:T(8,128)(2,1)} %all-gather.3.cloned.1.call-done, bf16[577,512]{0,1:T(8,128)(2,1)S(1)} %bitcast.111, bf16[577,512]{0,1:T(8,128)(2,1)S(1)} %bitcast.116, bf16[577,512]{0,1:T(8,128)(2,1)S(1)} %bitcast.97), kind=kOutput, calls=%fused_computation.51 | convolution fusion | flops 1820402688 | bytes 7281664 | tf_op jit(solution)/shard_map/te,de->td/dot_general | solution.py:265
  319.0 3.1 fusion.23
  322.0 17.7 %all-to-all-done.2 = bf16[8,64,2048]{2,1,0:T(8,128)(2,1)} async-done(((bf16[8,64,2048]{2,1,0:T(8,128)(2,1)}), bf16[8,64,2048]{2,1,0:T(8,128)(2,1)}, u32[]{:S(2)}, u32[]{:S(2)}) %all-to-all-start.2) | async-done | bytes 2097184 | tf_op jit(solution)/shard_map/all_to_all | solution.py:85
  339.7 3.8 all-to-all-start
  343.5 2.3 fusion.51
  347.6 2.8 convert_reduce_fusion.1
  352.4 4.5 %collective-permute-done.16 = f32[6144]{0:T(1024)S(1)} collective-permute-done((f32[6144]{0:T(1024)S(1)}, f32[6144]{0:T(1024)S(1)}, u32[]{:S(2)}, u32[]{:S(2)}) %collective-permute-start.16) | collective-permute-done | bytes 24608 | tf_op jit(solution)/shard_map/ppermute | solution.py:93
  358.6 11.9 %collective-permute-done.17 = f32[6144]{0:T(1024)S(1)} collective-permute-done((f32[6144]{0:T(1024)S(1)}, f32[6144]{0:T(1024)S(1)}, u32[]{:S(2)}, u32[]{:S(2)}) %collective-permute-start.17) | collective-permute-done | bytes 24608 | tf_op jit(solution)/shard_map/ppermute | solution.py:93
  370.5 3.7 collective-permute-start.18
  375.7 5.9 %collective-permute-done.18 = f32[6144]{0:T(1024)S(1)} collective-permute-done((f32[6144]{0:T(1024)S(1)}, f32[6144]{0:T(1024)S(1)}, u32[]{:S(2)}, u32[]{:S(2)}) %collective-permute-start.18) | collective-permute-done | bytes 24608 | tf_op jit(solution)/shard_map/ppermute | solution.py:93
  384.2 2.8 convert_reduce_fusion.2
  (203 shorter events, 70.4 us)
Async XLA Ops:
  7.2 9.8 %copy-start.26 = (f32[512]{0:T(512)S(1)}, f32[512]{0:T(512)}, u32[]{:S(2)}) copy-start(f32[512]{0:T(512)} %param.15) | copy-start | bytes 6148
  7.2 9.8 %copy-start.31 = (f32[512]{0:T(512)S(1)}, f32[512]{0:T(512)}, u32[]{:S(2)}) copy-start(f32[512]{0:T(512)} %param.16) | copy-start | bytes 6148
  7.2 56.7 %all-gather.3.cloned.1.call-start = ((), (), s32[]{:S(2)}) async-start(), calls=%async_computation.4 | async-start | bytes 4456448 | tf_op jit(solution)/shard_map/all_gather | solution.py:69
  8.2 11.2 %copy-start.29 = (f32[2,512]{1,0:T(2,128)S(1)}, f32[2,512]{1,0:T(2,128)}, u32[]{:S(2)}) copy-start(f32[2,512]{1,0:T(2,128)} %param.18) | copy-start | bytes 12292
  9.8 129.7 %all-gather.5.cloned.1.call-start = ((), (), s32[]{:S(2)}) async-start(), calls=%async_computation.5 | async-start | bytes 8912896 | tf_op jit(solution)/shard_map/all_gather | solution.py:69
  12.1 4.7 %collective-permute-start = (f32[2,577]{1,0:T(2,128)S(1)}, f32[2,577]{1,0:T(2,128)S(1)}, u32[]{:S(2)}, u32[]{:S(2)}) collective-permute-start(f32[2,577]{1,0:T(2,128)S(1)} %pad_maximum_fusion.3), channel_id=1, source_target_pairs={{0,1},{1,0},{2,3},{3,2},{4,5},{5,4},{6,7},{7,6},{8,9},{9,8},{10,11... | collective-permute-start | bytes 13856 | tf_op jit(solution)/shard_map/ppermute | solution.py:20
  17.4 14.4 %collective-permute-start.1 = (bf16[577,512]{1,0:T(8,128)(2,1)S(1)}, bf16[577,512]{1,0:T(8,128)(2,1)S(1)}, u32[]{:S(2)}, u32[]{:S(2)}) collective-permute-start(bf16[577,512]{1,0:T(8,128)(2,1)S(1)} %get-tuple-element.143), channel_id=1, source_target_pairs={{0,1},{1,0},{2,3},{3,2},{4,5},{5,4},{6,7},{7,6},{8,9},{9,8},{10,11... | collective-permute-start | bytes 1772552 | tf_op jit(solution)/shard_map/ppermute | solution.py:52
  31.9 32.0 %copy-start.20 = (bf16[577,1024]{1,0:T(8,128)(2,1)}, bf16[577,1024]{1,0:T(8,128)(2,1)S(1)}, u32[]{:S(2)}) copy-start(bf16[577,1024]{1,0:T(8,128)(2,1)S(1)} %constant_dynamic-update-slice_fusion.6) | copy-start | bytes 3545092
  80.9 18.7 %copy-start.12 = (bf16[8,64,577]{2,1,0:T(8,128)(2,1)}, bf16[8,64,577]{2,1,0:T(8,128)(2,1)S(1)}, u32[]{:S(2)}) copy-start(bf16[8,64,577]{2,1,0:T(8,128)(2,1)S(1)} %fusion.38) | copy-start | bytes 1772548
  80.9 18.3 %copy-start.30 = (f32[512]{0:T(512)S(1)}, f32[512]{0:T(512)}, u32[]{:S(2)}) copy-start(f32[512]{0:T(512)} %param.20) | copy-start | bytes 6148
  83.4 21.3 %copy-start.28 = (f32[512]{0:T(512)S(1)}, f32[512]{0:T(512)}, u32[]{:S(2)}) copy-start(f32[512]{0:T(512)} %param.21) | copy-start | bytes 6148
  83.4 21.3 %copy-start.32 = (f32[512]{0:T(512)S(1)}, f32[512]{0:T(512)}, u32[]{:S(2)}) copy-start(f32[512]{0:T(512)} %param.22) | copy-start | bytes 6148
  83.5 15.7 %collective-permute-start.2 = (bf16[577,512]{1,0:T(8,128)(2,1)S(1)}, bf16[577,512]{1,0:T(8,128)(2,1)S(1)}, u32[]{:S(2)}, u32[]{:S(2)}) collective-permute-start(bf16[577,512]{1,0:T(8,128)(2,1)S(1)} %dynamic-slice_convert_fusion.6), channel_id=1, source_target_pairs={{0,1},{1,0},{2,3},{3,2},{4,5},{5,4},{6,7},{7,6},{8,9},{9,8},{10,11... | collective-permute-start | bytes 1772552 | tf_op jit(solution)/shard_map/ppermute | solution.py:63
  99.7 3.7 collective-permute-start.3
  101.2 16.7 %collective-permute-start.6 = (bf16[577,512]{1,0:T(8,128)(2,1)}, bf16[577,512]{1,0:T(8,128)(2,1)}, u32[]{:S(2)}, u32[]{:S(2)}) collective-permute-start(bf16[577,512]{1,0:T(8,128)(2,1)} %param.27), channel_id=1, source_target_pairs={{0,1},{1,0},{2,3},{3,2},{4,5},{5,4},{6,7},{7,6},{8,9},{9,8},{10,11... | collective-permute-start | bytes 1772552 | tf_op jit(solution)/shard_map/ppermute | solution.py:52
  104.7 34.8 %copy-start.34 = (f32[2048]{0:T(1024)S(1)}, f32[2048]{0:T(1024)}, u32[]{:S(2)}) copy-start(f32[2048]{0:T(1024)} %param.24) | copy-start | bytes 24580
  105.9 23.0 %collective-permute-start.4 = (bf16[577,512]{1,0:T(8,128)(2,1)}, bf16[577,512]{1,0:T(8,128)(2,1)}, u32[]{:S(2)}, u32[]{:S(2)}) collective-permute-start(bf16[577,512]{1,0:T(8,128)(2,1)} %get-tuple-element.140), channel_id=1, source_target_pairs={{0,1},{1,0},{2,3},{3,2},{4,5},{5,4},{6,7},{7,6},{8,9},{9,8},{10,11... | collective-permute-start | bytes 1772552 | tf_op jit(solution)/shard_map/ppermute | solution.py:52
  166.1 9.8 %collective-permute-start.7 = (bf16[8,64,2048]{2,1,0:T(8,128)(2,1)}, bf16[8,64,2048]{2,1,0:T(8,128)(2,1)}, u32[]{:S(2)}, u32[]{:S(2)}) collective-permute-start(bf16[8,64,2048]{2,1,0:T(8,128)(2,1)} %fusion.28), channel_id=1, source_target_pairs={{0,2},{2,0},{4,6},{6,4},{8,10},{10,8},{12,14},{14,12},{16,18},{18,... | collective-permute-start | bytes 6291464 | tf_op jit(solution)/shard_map/ppermute | solution.py:78
  166.4 9.5 %copy-start.9 = (f32[1024,2048]{1,0:T(8,128)S(1)}, f32[1024,2048]{1,0:T(8,128)}, u32[]{:S(2)}) copy-start(f32[1024,2048]{1,0:T(8,128)} %copy-done.8) | copy-start | bytes 25165828
  175.9 14.8 %copy-start.15 = (bf16[577,2048]{1,0:T(8,128)(2,1)}, bf16[577,2048]{1,0:T(8,128)(2,1)S(1)}, u32[]{:S(2)}) copy-start(bf16[577,2048]{1,0:T(8,128)(2,1)S(1)} %add_convert_fusion) | copy-start | bytes 7090180
  175.9 14.8 %slice-start.2 = ((s8[8388608]{0:T(1024)(128)(4,1)}), s8[4194304]{0:T(1024)(128)(4,1)S(1)}, s32[]{:S(2)}) async-start(s8[8388608]{0:T(1024)(128)(4,1)} %bitcast.128), calls=%async_computation.8 | async-start | bytes 8388608
  180.5 10.1 %slice-start.3 = ((s8[8388608]{0:T(1024)(128)(4,1)}), s8[4194304]{0:T(1024)(128)(4,1)S(1)}, s32[]{:S(2)}) async-start(s8[8388608]{0:T(1024)(128)(4,1)} %bitcast.128), calls=%async_computation.9 | async-start | bytes 8388608
  190.4 35.9 %collective-permute-start.10 = (bf16[8,64,2048]{2,1,0:T(8,128)(2,1)}, bf16[8,64,2048]{2,1,0:T(8,128)(2,1)}, u32[]{:S(2)}, u32[]{:S(2)}) collective-permute-start(bf16[8,64,2048]{2,1,0:T(8,128)(2,1)} %fusion.29), channel_id=1, source_target_pairs={{0,2},{2,0},{4,6},{6,4},{8,10},{10,8},{12,14},{14,12},{16,18},{18,... | collective-permute-start | bytes 6291464 | tf_op jit(solution)/shard_map/ppermute | solution.py:78
  193.7 16.4 %collective-permute-start.8 = (bf16[577,512]{1,0:T(8,128)(2,1)S(1)}, bf16[577,512]{1,0:T(8,128)(2,1)S(1)}, u32[]{:S(2)}, u32[]{:S(2)}) collective-permute-start(bf16[577,512]{1,0:T(8,128)(2,1)S(1)} %dynamic-slice_convert_fusion.4), channel_id=1, source_target_pairs={{0,1},{1,0},{2,3},{3,2},{4,5},{5,4},{6,7},{7,6},{8,9},{9,8},{10,11... | collective-permute-start | bytes 1772552 | tf_op jit(solution)/shard_map/ppermute | solution.py:63
  197.9 13.7 %copy-start.19 = (f32[577,1024]{1,0:T(8,128)}, f32[577,1024]{1,0:T(8,128)S(1)}, u32[]{:S(2)}) copy-start(f32[577,1024]{1,0:T(8,128)S(1)} %fusion.17) | copy-start | bytes 7090180
  199.0 23.5 %collective-permute-start.5 = (bf16[577,512]{1,0:T(8,128)(2,1)}, bf16[577,512]{1,0:T(8,128)(2,1)}, u32[]{:S(2)}, u32[]{:S(2)}) collective-permute-start(bf16[577,512]{1,0:T(8,128)(2,1)} %dynamic-slice_convert_fusion.5), channel_id=1, source_target_pairs={{0,1},{1,0},{2,3},{3,2},{4,5},{5,4},{6,7},{7,6},{8,9},{9,8},{10,11... | collective-permute-start | bytes 1772552 | tf_op jit(solution)/shard_map/ppermute | solution.py:63
  211.7 10.8 %copy-start.33 = (f32[512]{0:T(512)S(1)}, f32[512]{0:T(512)}, u32[]{:S(2)}) copy-start(f32[512]{0:T(512)} %param.26) | copy-start | bytes 6148
  211.7 10.7 %collective-permute-start.9 = (f32[2,577]{1,0:T(2,128)S(1)}, f32[2,577]{1,0:T(2,128)S(1)}, u32[]{:S(2)}, u32[]{:S(2)}) collective-permute-start(f32[2,577]{1,0:T(2,128)S(1)} %pad_maximum_fusion.5), channel_id=1, source_target_pairs={{0,1},{1,0},{2,3},{3,2},{4,5},{5,4},{6,7},{7,6},{8,9},{9,8},{10,11... | collective-permute-start | bytes 13856 | tf_op jit(solution)/shard_map/ppermute | solution.py:20
  213.3 54.2 %all-to-all-start.3 = ((bf16[8,64,2048]{2,1,0:T(8,128)(2,1)}), bf16[8,64,2048]{2,1,0:T(8,128)(2,1)}, u32[]{:S(2)}, u32[]{:S(2)}) async-start(bf16[8,64,2048]{2,1,0:T(8,128)(2,1)} %fusion.14), calls=%async_computation.3 | async-start | bytes 4194304 | tf_op jit(solution)/shard_map/all_to_all | solution.py:85
  231.4 14.9 %collective-permute-start.11 = (bf16[577,512]{1,0:T(8,128)(2,1)S(1)}, bf16[577,512]{1,0:T(8,128)(2,1)S(1)}, u32[]{:S(2)}, u32[]{:S(2)}) collective-permute-start(bf16[577,512]{1,0:T(8,128)(2,1)S(1)} %get-tuple-element.66), channel_id=1, source_target_pairs={{0,1},{1,0},{2,3},{3,2},{4,5},{5,4},{6,7},{7,6},{8,9},{9,8},{10,11... | collective-permute-start | bytes 1772552 | tf_op jit(solution)/shard_map/ppermute | solution.py:52
  250.4 2.9 collective-permute-start.12
  267.5 19.2 %all-to-all-start.1 = ((bf16[8,64,512]{2,1,0:T(8,128)(2,1)}), bf16[8,64,512]{2,1,0:T(8,128)(2,1)S(1)}, u32[]{:S(2)}, u32[]{:S(2)}) async-start(bf16[8,64,512]{2,1,0:T(8,128)(2,1)} %fusion.54), calls=%async_computation.1 | async-start | bytes 1048576 | tf_op jit(solution)/shard_map/all_to_all | solution.py:85
  286.7 53.0 %all-to-all-start.2 = ((bf16[8,64,2048]{2,1,0:T(8,128)(2,1)}), bf16[8,64,2048]{2,1,0:T(8,128)(2,1)}, u32[]{:S(2)}, u32[]{:S(2)}) async-start(bf16[8,64,2048]{2,1,0:T(8,128)(2,1)} %fusion.13), calls=%async_computation.2 | async-start | bytes 4194304 | tf_op jit(solution)/shard_map/all_to_all | solution.py:85
  309.2 9.7 %collective-permute-start.19 = (bf16[8,64,1536]{2,1,0:T(8,128)(2,1)}, bf16[8,64,1536]{2,1,0:T(8,128)(2,1)}, u32[]{:S(2)}, u32[]{:S(2)}) collective-permute-start(bf16[8,64,1536]{2,1,0:T(8,128)(2,1)} %fusion.32), channel_id=1, source_target_pairs={{0,2},{2,0},{4,6},{6,4},{8,10},{10,8},{12,14},{14,12},{16,18},{18,... | collective-permute-start | bytes 4718600 | tf_op jit(solution)/shard_map/ppermute | solution.py:78
  311.3 7.6 %slice-start = ((s8[6291456]{0:T(1024)(128)(4,1)}), s8[4194304]{0:T(1024)(128)(4,1)S(1)}, s32[]{:S(2)}) async-start(s8[6291456]{0:T(1024)(128)(4,1)} %bitcast.105), calls=%async_computation.6 | async-start | bytes 8388608
  311.5 7.5 %slice-start.1 = ((s8[6291456]{0:T(1024)(128)(4,1)}), s8[2097152]{0:T(1024)(128)(4,1)S(1)}, s32[]{:S(2)}) async-start(s8[6291456]{0:T(1024)(128)(4,1)} %bitcast.105), calls=%async_computation.7 | async-start | bytes 4194304
  317.0 26.5 %collective-permute-start.13 = (bf16[577,512]{1,0:T(8,128)(2,1)}, bf16[577,512]{1,0:T(8,128)(2,1)}, u32[]{:S(2)}, u32[]{:S(2)}) collective-permute-start(bf16[577,512]{1,0:T(8,128)(2,1)} %dynamic-slice_convert_fusion.3), channel_id=1, source_target_pairs={{0,1},{1,0},{2,3},{3,2},{4,5},{5,4},{6,7},{7,6},{8,9},{9,8},{10,11... | collective-permute-start | bytes 1772552 | tf_op jit(solution)/shard_map/ppermute | solution.py:63
  322.0 21.5 %copy-start.23 = (f32[577]{0:T(1024)S(1)}, f32[577]{0:T(1024)}, u32[]{:S(2)}) copy-start(f32[577]{0:T(1024)} %copy-done.22) | copy-start | bytes 6928
  322.0 21.5 %copy-start.25 = (f32[577]{0:T(1024)S(1)}, f32[577]{0:T(1024)}, u32[]{:S(2)}) copy-start(f32[577]{0:T(1024)} %copy-done.24) | copy-start | bytes 6928
  322.0 21.5 %copy-start.27 = (f32[512]{0:T(512)S(1)}, f32[512]{0:T(512)}, u32[]{:S(2)}) copy-start(f32[512]{0:T(512)} %param.15) | copy-start | bytes 6148
  339.7 47.2 %all-to-all-start = ((bf16[8,64,1536]{2,1,0:T(8,128)(2,1)}), bf16[8,64,1536]{2,1,0:T(8,128)(2,1)S(1)}, u32[]{:S(2)}, u32[]{:S(2)}) async-start(bf16[8,64,1536]{2,1,0:T(8,128)(2,1)} %fusion.23), calls=%async_computation | async-start | bytes 3145728 | tf_op jit(solution)/shard_map/all_to_all | solution.py:85
  343.5 30.7 %copy-start.6 = (f32[577,512]{1,0:T(8,128)S(1)}, f32[577,512]{1,0:T(8,128)}, u32[]{:S(2)}) copy-start(f32[577,512]{1,0:T(8,128)} %get-tuple-element.135) | copy-start | bytes 3545092
  345.9 4.5 %collective-permute-start.15 = (f32[6144]{0:T(1024)S(1)}, f32[6144]{0:T(1024)S(1)}, u32[]{:S(2)}, u32[]{:S(2)}) collective-permute-start(f32[6144]{0:T(1024)S(1)} %constant_dynamic-update-slice_fusion.8), channel_id=1, source_target_pairs={{0,2},{2,0},{4,6},{6,4},{8,10},{10,8},{12,14},{14,12},{16,18},{18,... | collective-permute-start | bytes 73736 | tf_op jit(solution)/shard_map/ppermute | solution.py:93
  346.0 37.4 %copy-start.17 = (bf16[8,64,512]{2,1,0:T(8,128)(2,1)S(1)}, bf16[8,64,512]{2,1,0:T(8,128)(2,1)}, u32[]{:S(2)}) copy-start(bf16[8,64,512]{2,1,0:T(8,128)(2,1)} %copy-done.16) | copy-start | bytes 1572868
  346.0 6.4 %collective-permute-start.14 = (f32[2,577]{1,0:T(2,128)S(1)}, f32[2,577]{1,0:T(2,128)S(1)}, u32[]{:S(2)}, u32[]{:S(2)}) collective-permute-start(f32[2,577]{1,0:T(2,128)S(1)} %pad_maximum_fusion.6), channel_id=1, source_target_pairs={{0,1},{1,0},{2,3},{3,2},{4,5},{5,4},{6,7},{7,6},{8,9},{9,8},{10,11... | collective-permute-start | bytes 13856 | tf_op jit(solution)/shard_map/ppermute | solution.py:20
  350.4 6.5 %collective-permute-start.16 = (f32[6144]{0:T(1024)S(1)}, f32[6144]{0:T(1024)S(1)}, u32[]{:S(2)}, u32[]{:S(2)}) collective-permute-start(f32[6144]{0:T(1024)S(1)} %add.255), channel_id=1, source_target_pairs={{0,4},{2,6},{4,0},{6,2},{8,12},{10,14},{12,8},{14,10},{16,20},{18,... | collective-permute-start | bytes 73736 | tf_op jit(solution)/shard_map/ppermute | solution.py:93
  356.9 13.6 %collective-permute-start.17 = (f32[6144]{0:T(1024)S(1)}, f32[6144]{0:T(1024)S(1)}, u32[]{:S(2)}, u32[]{:S(2)}) collective-permute-start(f32[6144]{0:T(1024)S(1)} %add.256), channel_id=1, source_target_pairs={{0,8},{2,10},{4,12},{6,14},{8,0},{10,2},{12,4},{14,6},{16,24},{18,... | collective-permute-start | bytes 73736 | tf_op jit(solution)/shard_map/ppermute | solution.py:93
  370.5 11.1 %collective-permute-start.18 = (f32[6144]{0:T(1024)S(1)}, f32[6144]{0:T(1024)S(1)}, u32[]{:S(2)}, u32[]{:S(2)}) collective-permute-start(f32[6144]{0:T(1024)S(1)} %add.257), channel_id=1, source_target_pairs={{0,16},{2,18},{4,20},{6,22},{8,24},{10,26},{12,28},{14,30},{16,0},... | collective-permute-start | bytes 73736 | tf_op jit(solution)/shard_map/ppermute | solution.py:93
  (19 other events, 83.7 us)
Sparse Core Ops, SparseCore 0:
  10.8 53.0 all-gather.2
  66.6 72.8 all-gather.4
